TPU v7x, 32 devices: a whole 2x2x4 slice. The times are simulated.
32 devices in a mesh: seq: 8 (over z, y), head: 4 (over x, core).
Axes of the slice: x: 2, y: 2, z: 4, core: 2. Of those that a mesh axis runs over, the one named last changes fastest.
Arguments:
- queries: float32 [1024, 2048], P('seq', 'head'), may hold values from -6 to 6
- keys: float32 [1024, 2048], P('seq', 'head'), may hold values from -6 to 6
- values: float32 [1024, 2048], P('seq', 'head'), may hold values from -6 to 6
- rates: float32 [4, 1024], P('head', 'seq'), may hold values from 0.05 to 1
- gate_fast: float32 [4, 512, 512], P('head'), may hold values from -0.25 to 0.25
- up_fast: float32 [4, 512, 512], P('head'), may hold values from -0.25 to 0.25
- down_fast: float32 [4, 512, 512], P('head'), may hold values from -0.25 to 0.25
- out_proj: bfloat16 [2048, 4096], P('head', 'seq'), may hold values from -0.125 to 0.125
- out_grad: bfloat16 [1024, 4096], P('seq', 'head'), may hold values from -6 to 6
Outputs:
- query_grad: float32 [1024, 2048], P('seq', 'head')
- key_grad: float32 [1024, 2048], P('seq', 'head')
- value_grad: float32 [1024, 2048], P('seq', 'head')
- gate_grad: float32 [4, 512, 512], P('head', 'seq')
- up_grad: float32 [4, 512, 512], P('head', 'seq')
- down_grad: float32 [4, 512, 512], P('head', 'seq')
All inputs are finite; a program needn't handle non-finite values.
Results may differ from a plain program's by a relative error of at most 0.0003.
Values may be sent and summed in bfloat16 or wider, within the bound.
No kernel may reach another device: no remote copies, remote signals or barrier semaphores. Data moves between devices by JAX's collectives and lax.ppermute only.
A program may use at most 64 MiB of HBM per device.

v0:
```python
import math

import jax
import jax.numpy as jnp
from jax import lax
from jax.sharding import PartitionSpec as P


def matmul(left, right):
    return jnp.dot(left, right, precision=lax.Precision.HIGHEST, preferred_element_type=jnp.float32)


def swiglu(gate_matrix, up_matrix, down_matrix, inputs):
    before = matmul(inputs, gate_matrix.T)
    linear = matmul(inputs, up_matrix.T)
    hidden = jax.nn.silu(before) * linear
    return matmul(hidden, down_matrix.T)


def update_terms(gate_matrix, up_matrix, down_matrix, key_rows, value_rows, rate_rows):
    before = matmul(key_rows, gate_matrix.T)
    linear = matmul(key_rows, up_matrix.T)
    sigma = jax.nn.sigmoid(before)
    activated = before * sigma
    hidden = activated * linear
    target = -(rate_rows[:, None] * value_rows)
    term_down = matmul(target.T, hidden)
    hidden_grad = matmul(target, down_matrix)
    before_grad = hidden_grad * linear * sigma * (1.0 + before * (1.0 - sigma))
    linear_grad = hidden_grad * activated
    return (matmul(before_grad.T, key_rows), matmul(linear_grad.T, key_rows), term_down)


def renorm(weight, partial_value, total_sq, scale):
    norm_update = jnp.sqrt(total_sq + 1e-06)
    moved = weight - partial_value * (scale / norm_update)[..., None, None]
    norm_old = jnp.sqrt(jnp.sum(weight * weight, axis=-1) + 1e-06)
    norm_new = jnp.sqrt(jnp.sum(moved * moved, axis=-1) + 1e-06)
    return (moved * (norm_old / norm_new)[..., None], norm_new, norm_update)


def back_rows(weight, renormed, norm_new, grad, norm_update, scale):
    norm_old = jnp.sqrt(jnp.sum(weight * weight, axis=-1) + 1e-06)
    moved = renormed * (norm_new / norm_old)[..., None]
    partial_value = (weight - moved) * (norm_update / scale)[..., None, None]
    along = jnp.sum(moved * grad, axis=-1)
    moved_grad = (norm_old / norm_new)[..., None] * (
        grad - moved * (along / (norm_new * norm_new))[..., None]
    )
    direct = moved_grad + (along / (norm_new * norm_old))[..., None] * weight
    return (direct, -moved_grad, partial_value)


def step_back(step_grad, partial_value, inner, norm_update, scale):
    factor = inner / (norm_update * norm_update)
    return (scale / norm_update)[..., None, None] * (
        step_grad - partial_value * factor[..., None, None]
    )


def body(queries, keys, values, rates, gate_fast, up_fast, down_fast, out_proj, out_grad):
    tokens_here = queries.shape[0]
    heads_here = gate_fast.shape[0]
    head_size = gate_fast.shape[2]
    seq_count = lax.axis_size("seq")
    seq_index = lax.axis_index("seq")

    def split_heads(array):
        return array.reshape(tokens_here, heads_here, head_size).transpose(1, 0, 2)

    def join_heads(array):
        return array.transpose(1, 0, 2).reshape(tokens_here, heads_here * head_size)

    grad_full = lax.all_gather(out_grad, "head", axis=1, tiled=True)
    out_cot = lax.dot_general(
        grad_full,
        lax.all_gather(out_proj, "seq", axis=1, tiled=True),
        (((1,), (1,)), ((), ())),
        preferred_element_type=jnp.float32,
    )
    weights = (gate_fast, up_fast, down_fast)
    scales = tuple((0.3 * math.sqrt(matrix.shape[1]) for matrix in weights))
    share_rows = [matrix.shape[1] // seq_count for matrix in weights]

    def update_heads(gate_matrix, up_matrix, down_matrix, key_heads, value_heads):
        return jax.vmap(update_terms)(
            gate_matrix, up_matrix, down_matrix, key_heads, value_heads, rates
        )

    partials, update_pull = jax.vjp(
        update_heads, gate_fast, up_fast, down_fast, split_heads(keys), split_heads(values)
    )
    totals = lax.psum((partials[0], partials[1], partials[2]), "seq")
    normed = [
        renorm(
            weights[slot],
            totals[slot],
            jnp.sum(totals[slot] * totals[slot], axis=(1, 2)),
            scales[slot],
        )
        for slot in range(3)
    ]
    renormed = [normed[slot][0] for slot in range(3)]
    new_norms = [normed[slot][1] for slot in range(3)]
    update_norms = [normed[slot][2] for slot in range(3)]

    def apply_heads(gate_matrix, up_matrix, down_matrix, query_heads):
        return jax.vmap(swiglu)(gate_matrix, up_matrix, down_matrix, query_heads)

    applied, apply_pull = jax.vjp(
        apply_heads, renormed[0], renormed[1], renormed[2], split_heads(queries)
    )
    cot_gate, cot_up, cot_down, query_part = apply_pull(split_heads(out_cot))
    summed = lax.psum((cot_gate, cot_up, cot_down), "seq")
    backs = [
        back_rows(
            weights[slot],
            renormed[slot],
            new_norms[slot],
            summed[slot],
            update_norms[slot],
            scales[slot],
        )
        for slot in range(3)
    ]
    directions = [
        step_back(
            backs[slot][1],
            backs[slot][2],
            jnp.sum(backs[slot][2] * backs[slot][1], axis=(1, 2)),
            update_norms[slot],
            scales[slot],
        )
        for slot in range(3)
    ]
    directs = [
        lax.dynamic_slice_in_dim(backs[slot][0], seq_index * share_rows[slot], share_rows[slot], 1)
        for slot in range(3)
    ]
    through_gate, through_up, through_down, key_part, value_part = update_pull(
        (directions[0], directions[1], directions[2])
    )
    throughs = (
        lax.psum_scatter(through_gate, "seq", scatter_dimension=1, tiled=True),
        lax.psum_scatter(through_up, "seq", scatter_dimension=1, tiled=True),
        lax.psum_scatter(through_down, "seq", scatter_dimension=1, tiled=True),
    )
    return (
        join_heads(query_part),
        join_heads(key_part),
        join_heads(value_part),
        directs[0] + throughs[0],
        directs[1] + throughs[1],
        directs[2] + throughs[2],
    )


def solution(mesh):
    placed = (
        P("seq", "head"),
        P("seq", "head"),
        P("seq", "head"),
        P("head", "seq"),
        P("head", None, None),
        P("head", None, None),
        P("head", None, None),
        P("head", "seq"),
        P("seq", "head"),
    )
    return jax.shard_map(
        body,
        mesh=mesh,
        in_specs=placed,
        out_specs=(
            P("seq", "head"),
            P("seq", "head"),
            P("seq", "head"),
            P("head", "seq", None),
            P("head", "seq", None),
            P("head", "seq", None),
        ),
        check_vma=False,
    )
```

profile of v0, /device:TPU:0, one launch (start us, length us, event | category | flops | bytes accessed | tf_op | source)
XLA Modules:
  0.0 572.3 jit_solution(3164507224037703862)
XLA Ops:
  9.0 2.4 fusion.23
  11.4 2.5 fusion.26
  13.9 2.1 fusion.29
  18.0 2.1 convolution_bitcast_fusion.7
  20.1 2.1 convolution_bitcast_fusion.8
  23.6 160.0 %all-reduce.7.cloned.1.call-done = (f32[1,512,512]{2,1,0:T(8,128)}, f32[1,512,512]{2,1,0:T(8,128)}, f32[1,512,512]{2,1,0:T(8,128)}) async-done(((f32[1,512,512]{2,1,0:T(8,128)}, f32[1,512,512]{2,1,0:T(8,128)}, f32[1,512,512]{2,1,0:T(8,128)}), (f32[1,512,512]{2,1,0:T(8,128)}, f32[1,512,512]{2,1,0:T(8,128)}, f32[1,512,512]{2,1,0:T(8,128)})) %all-reduce.7.cloned.1.call-update) | async-done | bytes 3145744 | tf_op jit(solution)/shard_map/psum | solution.py:93
  183.7 2.1 multiply_reduce_fusion.8
  186.5 2.2 multiply_reduce_fusion.11
  189.5 2.1 multiply_reduce_fusion.14
  192.3 3.3 multiply_reduce_fusion.6
  199.2 2.0 convolution_bitcast_fusion.16
  201.3 4.2 fusion.88
  206.3 2.1 convolution_bitcast_fusion.3
  208.4 2.1 convolution_bitcast_fusion.4
  212.8 127.9 %all-reduce.5.cloned.1.call-done = (f32[1,512,512]{2,1,0:T(8,128)}, f32[1,512,512]{2,1,0:T(8,128)}, f32[1,512,512]{2,1,0:T(8,128)}) async-done(((f32[1,512,512]{2,1,0:T(8,128)}, f32[1,512,512]{2,1,0:T(8,128)}, f32[1,512,512]{2,1,0:T(8,128)}), (f32[1,512,512]{2,1,0:T(8,128)}, f32[1,512,512]{2,1,0:T(8,128)}, f32[1,512,512]{2,1,0:T(8,128)})) %all-reduce.5.cloned.1.call-update) | async-done | bytes 3145744 | tf_op jit(solution)/shard_map/psum | solution.py:114
  344.3 2.4 multiply_reduce_fusion.4
  347.4 3.5 multiply_reduce_fusion.2
  351.6 4.2 multiply_reduce_fusion
  356.5 3.0 convolution_bitcast_fusion.12
  359.5 2.9 convolution_bitcast_fusion.15
  365.1 2.1 convolution_bitcast_fusion.2
  367.2 3.0 convolution_bitcast_fusion.1
  370.6 3.1 convolution_bitcast_fusion
  373.8 2.0 fusion.16
  375.8 2.7 convolution_add_fusion.1
  378.6 2.9 convolution_bitcast_fusion.11
  385.3 2.5 fusion.3
  389.8 3.0 convolution_bitcast_fusion.9
  392.8 2.8 fusion.7
  395.7 34.9 %reduce-scatter.4.cloned.1.call-done = f32[1,64,512]{2,1,0:T(8,128)} async-done(((f32[1,512,512]{2,1,0:T(8,128)}), f32[1,64,512]{2,1,0:T(8,128)}) %reduce-scatter.4.cloned.1.call-update) | async-done | bytes 131088 | tf_op jit(solution)/shard_map/reduce_scatter | solution.py:144
  432.2 64.8 %reduce-scatter.6.cloned.1.call-done = f32[1,64,512]{2,1,0:T(8,128)} async-done(((f32[1,512,512]{2,1,0:T(8,128)}), f32[1,64,512]{2,1,0:T(8,128)}) %reduce-scatter.6.cloned.1.call-update) | async-done | bytes 131088 | tf_op jit(solution)/shard_map/reduce_scatter | solution.py:145
  498.8 64.7 %reduce-scatter.8.cloned.1.call-done = f32[1,64,512]{2,1,0:T(8,128)} async-done(((f32[1,512,512]{2,1,0:T(8,128)}), f32[1,64,512]{2,1,0:T(8,128)}) %reduce-scatter.8.cloned.1.call-update) | async-done | bytes 131088 | tf_op jit(solution)/shard_map/reduce_scatter | solution.py:146
  (110 shorter events, 28.6 us)
Async XLA Ops:
  8.0 10.0 %copy-start.30 = (f32[128,512]{1,0:T(8,128)S(1)}, f32[128,512]{1,0:T(8,128)}, u32[]{:S(2)}) copy-start(f32[128,512]{1,0:T(8,128)} %param.11) | copy-start | bytes 786436
  8.0 10.0 %copy-start.34 = (f32[1,128]{1,0:T(1,128)S(1)}, f32[1,128]{1,0:T(1,128)}, u32[]{:S(2)}) copy-start(f32[1,128]{1,0:T(1,128)} %param.12) | copy-start | bytes 1540
  8.0 175.6 %all-reduce.7.cloned.1.call-start = ((), (), s32[]{:S(2)}) async-start(), calls=%async_computation.9 | async-start | bytes 6291456 | tf_op jit(solution)/shard_map/psum | solution.py:93
  11.3 10.9 %copy-start.8 = (f32[128,512]{1,0:T(8,128)}, f32[128,512]{1,0:T(8,128)S(1)}, u32[]{:S(2)}) copy-start(f32[128,512]{1,0:T(8,128)S(1)} %fusion.23) | copy-start | bytes 786436
  13.8 8.4 %copy-start.21 = (f32[128,512]{1,0:T(8,128)}, f32[128,512]{1,0:T(8,128)S(1)}, u32[]{:S(2)}) copy-start(f32[128,512]{1,0:T(8,128)S(1)} %fusion.26) | copy-start | bytes 786436
  16.0 6.2 %copy-start.18 = (f32[128,512]{1,0:T(8,128)}, f32[128,512]{1,0:T(8,128)S(1)}, u32[]{:S(2)}) copy-start(f32[128,512]{1,0:T(8,128)S(1)} %fusion.29) | copy-start | bytes 786436
  20.1 172.2 %copy-start.2 = (f32[1,512,512]{2,1,0:T(8,128)S(1)}, f32[1,512,512]{2,1,0:T(8,128)}, u32[]{:S(2)}) copy-start(f32[1,512,512]{2,1,0:T(8,128)} %param.14) | copy-start | bytes 3145732
  22.2 179.0 %all-gather.3.cloned.1.call-start = ((), (), s32[]{:S(2)}) async-start(), calls=%async_computation.3 | async-start | bytes 1310720 | tf_op jit(solution)/shard_map/all_gather | solution.py:74
  22.8 178.4 %all-gather.5.cloned.1.call-start = ((), (), s32[]{:S(2)}) async-start(), calls=%async_computation.4 | async-start | bytes 4718592 | tf_op jit(solution)/shard_map/all_gather | solution.py:77
  23.4 317.3 %all-reduce.5.cloned.1.call-start = ((), (), s32[]{:S(2)}) async-start(), calls=%async_computation.8 | async-start | bytes 6291456 | tf_op jit(solution)/shard_map/psum | solution.py:114
  186.5 9.2 %copy-start.1 = (f32[1,512,512]{2,1,0:T(8,128)S(1)}, f32[1,512,512]{2,1,0:T(8,128)}, u32[]{:S(2)}) copy-start(f32[1,512,512]{2,1,0:T(8,128)} %param.13) | copy-start | bytes 3145732
  201.3 5.0 copy-start.29
  201.3 7.1 %copy-start.28 = (f32[128,512]{1,0:T(8,128)S(1)}, f32[128,512]{1,0:T(8,128)}, u32[]{:S(2)}) copy-start(f32[128,512]{1,0:T(8,128)} %param.9) | copy-start | bytes 786436
  212.5 218.0 %reduce-scatter.4.cloned.1.call-start = ((), (), s32[]{:S(2)}) async-start(), calls=%async_computation.5 | async-start | bytes 1179648 | tf_op jit(solution)/shard_map/reduce_scatter | solution.py:144
  356.4 6.0 %copy-start.9 = (f32[128,512]{1,0:T(8,128)S(1)}, f32[128,512]{1,0:T(8,128)}, u32[]{:S(2)}) copy-start(f32[128,512]{1,0:T(8,128)} %copy-done.8) | copy-start | bytes 786436
  356.4 6.0 %copy-start.13 = (f32[1,512,512]{2,1,0:T(8,128)S(1)}, f32[1,512,512]{2,1,0:T(8,128)}, u32[]{:S(2)}) copy-start(f32[1,512,512]{2,1,0:T(8,128)} %get-tuple-element.22) | copy-start | bytes 3145732
  356.4 6.0 %copy-start.16 = (f32[1,512,512]{2,1,0:T(8,128)S(1)}, f32[1,512,512]{2,1,0:T(8,128)}, u32[]{:S(2)}) copy-start(f32[1,512,512]{2,1,0:T(8,128)} %get-tuple-element.23) | copy-start | bytes 3145732
  356.5 6.0 %copy-start.19 = (f32[128,512]{1,0:T(8,128)S(1)}, f32[128,512]{1,0:T(8,128)}, u32[]{:S(2)}) copy-start(f32[128,512]{1,0:T(8,128)} %copy-done.18) | copy-start | bytes 786436
  356.5 6.0 %copy-start.22 = (f32[128,512]{1,0:T(8,128)S(1)}, f32[128,512]{1,0:T(8,128)}, u32[]{:S(2)}) copy-start(f32[128,512]{1,0:T(8,128)} %copy-done.21) | copy-start | bytes 786436
  356.5 6.0 %copy-start.31 = (f32[128,512]{1,0:T(8,128)S(1)}, f32[128,512]{1,0:T(8,128)}, u32[]{:S(2)}) copy-start(f32[128,512]{1,0:T(8,128)} %param.11) | copy-start | bytes 786436
  367.2 129.9 %reduce-scatter.6.cloned.1.call-start = ((), (), s32[]{:S(2)}) async-start(), calls=%async_computation.6 | async-start | bytes 1179648 | tf_op jit(solution)/shard_map/reduce_scatter | solution.py:145
  370.3 193.2 %reduce-scatter.8.cloned.1.call-start = ((), (), s32[]{:S(2)}) async-start(), calls=%async_computation.7 | async-start | bytes 1179648 | tf_op jit(solution)/shard_map/reduce_scatter | solution.py:146
  373.7 7.7 %copy-start.10 = (f32[128,512]{1,0:T(8,128)S(1)}, f32[128,512]{1,0:T(8,128)}, u32[]{:S(2)}) copy-start(f32[128,512]{1,0:T(8,128)} %copy-done.8) | copy-start | bytes 786436
  373.7 7.7 %copy-start.11 = (f32[1,512,512]{2,1,0:T(8,128)S(1)}, f32[1,512,512]{2,1,0:T(8,128)}, u32[]{:S(2)}) copy-start(f32[1,512,512]{2,1,0:T(8,128)} %get-tuple-element.19) | copy-start | bytes 3145732
  373.7 7.7 %copy-start.14 = (f32[1,512,512]{2,1,0:T(8,128)S(1)}, f32[1,512,512]{2,1,0:T(8,128)}, u32[]{:S(2)}) copy-start(f32[1,512,512]{2,1,0:T(8,128)} %get-tuple-element.20) | copy-start | bytes 3145732
  373.7 7.7 %copy-start.20 = (f32[128,512]{1,0:T(8,128)S(1)}, f32[128,512]{1,0:T(8,128)}, u32[]{:S(2)}) copy-start(f32[128,512]{1,0:T(8,128)} %copy-done.18) | copy-start | bytes 786436
  373.7 9.6 %copy-start.12 = (f32[1,512,512]{2,1,0:T(8,128)S(1)}, f32[1,512,512]{2,1,0:T(8,128)}, u32[]{:S(2)}) copy-start(f32[1,512,512]{2,1,0:T(8,128)} %get-tuple-element.25) | copy-start | bytes 3145732
  373.7 9.6 %copy-start.15 = (f32[1,512,512]{2,1,0:T(8,128)S(1)}, f32[1,512,512]{2,1,0:T(8,128)}, u32[]{:S(2)}) copy-start(f32[1,512,512]{2,1,0:T(8,128)} %get-tuple-element.26) | copy-start | bytes 3145732
  373.8 9.6 %copy-start.23 = (f32[128,512]{1,0:T(8,128)S(1)}, f32[128,512]{1,0:T(8,128)}, u32[]{:S(2)}) copy-start(f32[128,512]{1,0:T(8,128)} %copy-done.21) | copy-start | bytes 786436
  378.5 6.7 %copy-start.4 = (f32[1,512,512]{2,1,0:T(8,128)S(1)}, f32[1,512,512]{2,1,0:T(8,128)}, u32[]{:S(2)}) copy-start(f32[1,512,512]{2,1,0:T(8,128)} %param.14) | copy-start | bytes 3145732
  378.5 6.7 %copy-start.33 = (f32[1,128,512]{2,1,0:T(8,128)S(1)}, f32[1,128,512]{2,1,0:T(8,128)}, u32[]{:S(2)}) copy-start(f32[1,128,512]{2,1,0:T(8,128)} %get-tuple-element.35) | copy-start | bytes 786436
  383.3 9.5 %copy-start.5 = (f32[1,512,512]{2,1,0:T(8,128)S(1)}, f32[1,512,512]{2,1,0:T(8,128)}, u32[]{:S(2)}) copy-start(f32[1,512,512]{2,1,0:T(8,128)} %param.15) | copy-start | bytes 3145732
  (10 other events, 33.6 us)
Sparse Core Ops, SparseCore 0:
  22.3 161.2 all-reduce.6
  212.6 128.0 all-reduce.4
  367.3 63.1 reduce-scatter.3
  433.8 63.2 reduce-scatter.5
  500.3 63.1 reduce-scatter.7
Sparse Core Ops, SparseCore 1:
  24.3 19.3 all-gather.2
  45.5 85.6 all-gather.4
where the time goes:
time: 573 us; the launch traced here: 572 us
  waiting for transfers between devices  454 us (79%)
  matrix products  64.1 us (11%)
  other arithmetic  30 us (5%)
  between operations  20 us (3%)
    psum x1, waiting for transfers between devices, body(): totals = lax.psum((partials[0], partials[1], partials[2]), 'seq')  160 us
    psum x1, waiting for transfers between devices, body(): summed = lax.psum((cot_gate, cot_up, cot_down), 'seq')  128 us
    reduce_scatter x1, waiting for transfers between devices, body(): lax.psum_scatter(through_up, 'seq', scatter_dimension=1, tiled=True)  64.8 us
    reduce_scatter x1, waiting for transfers between devices, body(): lax.psum_scatter(through_down, 'seq', scatter_dimension=1, tiled=True)  64.7 us
    dot_general x26, matrix products, matmul(): jnp.dot(left, right, precision=lax.Precision.HIGHEST, preferred_element_t...  59.9 us
    reduce_scatter x1, waiting for transfers between devices, body(): lax.psum_scatter(through_gate, 'seq', scatter_dimension=1, tiled=True)  34.9 us
  transfers between devices with their start and end apart: 7, of which 5 were waited for; matrix products, arithmetic and copies ran while one was open for 8% of the time, Pallas kernels for 0%

commit v1 on v0

--- a/solution.py
+++ b/solution.py
@@ -3,6 +3,8 @@
 import jax
 import jax.numpy as jnp
 from jax import lax
+from jax.experimental import pallas as pl
+from jax.experimental.pallas import tpu as pltpu
 from jax.sharding import PartitionSpec as P
 
 
@@ -107,7 +109,7 @@
     def apply_heads(gate_matrix, up_matrix, down_matrix, query_heads):
         return jax.vmap(swiglu)(gate_matrix, up_matrix, down_matrix, query_heads)
 
-    applied, apply_pull = jax.vjp(
+    _, apply_pull = jax.vjp(
         apply_heads, renormed[0], renormed[1], renormed[2], split_heads(queries)
     )
     cot_gate, cot_up, cot_down, query_part = apply_pull(split_heads(out_cot))
@@ -155,6 +157,546 @@
     )
 
 
+OCTAVES = 240.0
+LANES = 128
+
+
+def split(rows):
+    high = rows.astype(jnp.bfloat16)
+    return high, (rows - high.astype(jnp.float32)).astype(jnp.bfloat16)
+
+
+def join(*pairs, axis):
+    return tuple(jnp.concatenate(side, axis=axis) for side in zip(*pairs))
+
+
+def dot3(left, right, dims):
+    def one(a, b):
+        return lax.dot_general(a, b, (dims, ((), ())), preferred_element_type=jnp.float32)
+
+    return one(left[0], right[0]) + (one(left[0], right[1]) + one(left[1], right[0]))
+
+
+NT = ((1,), (1,))
+NN = ((1,), (0,))
+TN = ((0,), (0,))
+
+
+def encode(*groups):
+    blocks, tiles = [], []
+    for rows in groups:
+        top = jnp.max(jnp.abs(rows), axis=1, keepdims=True)
+        scale = (top * 1.01 + 1e-30).astype(jnp.bfloat16).astype(jnp.float32)
+        slope = (OCTAVES * math.log(2.0)) / scale
+        code = jnp.exp(jnp.abs(rows) * slope - 0.5 * OCTAVES * math.log(2.0))
+        code = jnp.where(rows < 0, -code, code).astype(jnp.bfloat16)
+        blocks += [code[:, at : at + LANES] for at in range(0, rows.shape[1], LANES)]
+        spread = jnp.transpose(jnp.broadcast_to(scale, (rows.shape[0], LANES)))
+        tiles.append(spread[: 16 // len(groups)])
+    return blocks + [jnp.concatenate(tiles, axis=0).astype(jnp.bfloat16)]
+
+
+def put(ref, start, blocks):
+    for block in blocks:
+        ref[start : start + block.shape[0], :] = block
+        start += block.shape[0]
+    return start
+
+
+def decode(ref, start, rows, width, groups=1):
+    count = width // LANES
+    tile = ref[start + groups * count * rows : start + groups * count * rows + 16, :].astype(jnp.float32)
+    found = []
+    for group in range(groups):
+        line = tile[group * (16 // groups) : group * (16 // groups) + 1]
+        scale = jnp.transpose(jnp.broadcast_to(line, (LANES, rows)))
+        slope = scale * (1.0 / (OCTAVES * math.log(2.0)))
+        half = scale * 0.5
+        parts = []
+        for block in range(count):
+            at = start + (group * count + block) * rows
+            code = ref[at : at + rows, :].astype(jnp.float32)
+            size = jnp.log(jnp.abs(code)) * slope + half
+            parts.append(jnp.where(code < 0, -size, size))
+        found.append(jnp.concatenate(parts, axis=1))
+    return found
+
+
+def coded_rows(rows, width, groups=1):
+    return groups * (width // LANES) * rows + 16
+
+
+def column(row):
+    return jnp.transpose(jnp.broadcast_to(row, (LANES, row.shape[1])))[:, :1]
+
+
+def silu_parts(before):
+    sigma = 1.0 / (1.0 + jnp.exp(-before))
+    return sigma, before * sigma, sigma * (1.0 + before * (1.0 - sigma))
+
+
+def row_norm(matrix):
+    return jnp.sqrt(jnp.sum(matrix * matrix, axis=1, keepdims=True) + 1e-06)
+
+
+def call(kernel, shapes, *arrays, scratch=(), smem=0):
+    specs = [pl.BlockSpec(memory_space=pltpu.SMEM)] * smem
+    specs += [pl.BlockSpec(memory_space=pltpu.VMEM)] * (len(arrays) - smem)
+    return pl.pallas_call(
+        kernel,
+        out_shape=[jax.ShapeDtypeStruct(shape, dtype) for shape, dtype in shapes],
+        in_specs=specs,
+        out_specs=[pl.BlockSpec(memory_space=pltpu.VMEM)] * len(shapes),
+        scratch_shapes=list(scratch),
+    )(*arrays)
+
+
+def first_kernel(keys, values, rates, target, packed):
+    scaled = -(column(rates[...]) * values[...])
+    target[...] = scaled
+    put(packed, 0, encode(keys[...], scaled))
+
+
+def query_kernel(queries, down, packed, down_squares):
+    put(packed, 0, encode(queries[...]))
+    squares = jnp.sum(down[...] * down[...], axis=1, keepdims=True)
+    down_squares[...] = jnp.transpose(jnp.broadcast_to(squares, (squares.shape[0], LANES)))[:1]
+
+
+def body_hidden(queries, keys, values, rates, gate_fast, up_fast, down_fast, out_proj, out_grad):
+    heads = lax.axis_size("head")
+    seq_count = lax.axis_size("seq")
+    depth = seq_count // 2
+    place = lax.axis_index("seq")
+    along_z = place // 2
+    along_y = place % 2
+    my_head = lax.axis_index("head")
+    head_size = gate_fast.shape[2]
+    hidden_size = gate_fast.shape[1]
+    part = hidden_size // depth
+    tokens = queries.shape[0]
+    half = part // 2
+    f32, bf16 = jnp.float32, jnp.bfloat16
+    scales = tuple(0.3 * math.sqrt(matrix.shape[1]) for matrix in (gate_fast, up_fast, down_fast))
+    size_one = coded_rows(tokens, head_size)
+    size_two = coded_rows(tokens, head_size, 2)
+    size_part = coded_rows(part, head_size)
+    steps = range(1, depth)
+
+    def turn(array, step):
+        perm = [(s, (s + 2 * step) % seq_count) for s in range(seq_count)]
+        return lax.ppermute(array, "seq", perm)
+
+    def swap(array):
+        return lax.ppermute(array, "seq", [(s, s ^ 1) for s in range(seq_count)])
+
+    def gather_z(packed):
+        return [turn(packed, step) for step in steps]
+
+    def scatter_z(slots):
+        return [turn(packed, -step) for step, packed in zip(steps, slots)]
+
+    def sum_z(array):
+        reach = 1
+        while True:
+            other = lax.ppermute(array, "seq", [(s, s ^ (2 * reach)) for s in range(seq_count)])
+            reach *= 2
+            if reach >= depth:
+                return array, other
+            array = array + other
+
+    target, kv_packed = call(
+        first_kernel, [((tokens, head_size), f32), ((size_two, LANES), bf16)], keys, values, rates
+    )
+    kv_sent = gather_z(kv_packed)
+
+    perm = []
+    for s in range(seq_count):
+        z, y = divmod(s, 2)
+        lane = (2 * z + z // (heads // 2)) % heads
+        perm += [(s * heads + h, (2 * h + y) * heads + lane) for h in range(heads)]
+    og_mine = lax.ppermute(out_grad, ("seq", "head"), perm)
+    op_other = swap(out_proj)
+    og_all = [og_mine] + [
+        lax.ppermute(og_mine, "head", [(h, (h + step) % heads) for h in range(heads)])
+        for step in range(1, heads)
+    ]
+
+    def contract_kernel(spot, mine, other, *refs):
+        rows, outs, product = refs[:heads], refs[heads:-1], refs[-1]
+        z, y, h = spot[0], spot[1], spot[2]
+        width = mine.shape[1]
+        for k in range(heads):
+            first = rows[k][:, pl.ds(pl.multiple_of(y * width, width), width)]
+            second = rows[k][:, pl.ds(pl.multiple_of((1 - y) * width, width), width)]
+            block = lax.dot_general(first, mine[...], (NT, ((), ())), preferred_element_type=f32)
+            block = block + lax.dot_general(second, other[...], (NT, ((), ())), preferred_element_type=f32)
+            lane = lax.rem(h - k + heads, heads)
+            source = lax.div(lane, 2) + lax.rem(lane, 2) * (heads // 2)
+            slot = lax.rem(z - source + depth, depth)
+            product[pl.ds(pl.multiple_of(slot * tokens, tokens), tokens), :] = block
+        outs[0][...] = product[:tokens, :]
+        for step in steps:
+            put(outs[step], 0, encode(product[step * tokens : (step + 1) * tokens, :]))
+
+    spot = jnp.stack([along_z, along_y, my_head]).astype(jnp.int32)
+    oc_own, *oc_slots = call(
+        contract_kernel,
+        [((tokens, head_size), f32)] + [((size_one, LANES), bf16)] * (depth - 1),
+        spot,
+        out_proj,
+        op_other,
+        *og_all,
+        scratch=[pltpu.VMEM((depth * tokens, head_size), f32)],
+        smem=1,
+    )
+    oc_back = scatter_z(oc_slots)
+
+    def total_kernel(own, *refs):
+        sent, (total, packed) = refs[: depth - 1], refs[depth - 1 :]
+        value = own[...]
+        for ref in sent:
+            value = value + decode(ref, 0, tokens, head_size)[0]
+        total[...] = value
+        put(packed, 0, encode(value))
+
+    out_cot, oc_packed = call(
+        total_kernel, [((tokens, head_size), f32), ((size_one, LANES), bf16)], oc_own, *oc_back
+    )
+    oc_sent = gather_z(oc_packed)
+    q_packed, down_sq = call(
+        query_kernel, [((size_one, LANES), bf16), ((1, head_size), f32)], queries, down_fast[0]
+    )
+    q_sent = gather_z(q_packed)
+
+    start = along_z * part
+    gate = lax.dynamic_slice_in_dim(gate_fast[0], start, part, 0)
+    up = lax.dynamic_slice_in_dim(up_fast[0], start, part, 0)
+    down = lax.dynamic_slice_in_dim(down_fast[0], start, part, 1).T
+    weights = jnp.concatenate([gate, up, down], axis=0)
+
+    def update_kernel(weight, key_own, target_own, *refs):
+        sent = refs[: depth - 1]
+        key_high, key_low, target_high, target_low, mids, partial, packed = refs[depth - 1 :]
+        two = split(weight[: 2 * part, :])
+        third = split(weight[2 * part :, :])
+        sum_two = jnp.zeros((2 * part, head_size), f32)
+        sum_one = jnp.zeros((part, head_size), f32)
+        for slot in range(depth):
+            at = slot * tokens
+            if slot == 0:
+                key_rows, target_rows = key_own[...], target_own[...]
+            else:
+                key_rows, target_rows = decode(sent[slot - 1], 0, tokens, head_size, 2)
+            key_rows, target_rows = split(key_rows), split(target_rows)
+            key_high[at : at + tokens, :], key_low[at : at + tokens, :] = key_rows
+            target_high[at : at + tokens, :], target_low[at : at + tokens, :] = target_rows
+            both = dot3(key_rows, two, NT)
+            hgrad = dot3(target_rows, third, NT)
+            mids[at : at + tokens, : 2 * part] = both
+            mids[at : at + tokens, 2 * part :] = hgrad
+            before, linear = both[:, :part], both[:, part:]
+            _, act, slope = silu_parts(before)
+            grads = split(jnp.concatenate([hgrad * linear * slope, hgrad * act], axis=1))
+            sum_two = sum_two + dot3(grads, key_rows, TN)
+            sum_one = sum_one + dot3(split(act * linear), target_rows, TN)
+        partial[: 2 * part, :] = sum_two
+        partial[2 * part :, :] = sum_one
+        end = put(packed, 0, encode(sum_two[:part]))
+        end = put(packed, end, encode(sum_two[part:]))
+        put(packed, end, encode(sum_one))
+
+    *kv_split, mids, partial_own, partial_packed = call(
+        update_kernel,
+        [((depth * tokens, head_size), bf16)] * 4
+        + [((depth * tokens, 3 * part), f32), ((3 * part, head_size), f32), ((3 * size_part, LANES), bf16)],
+        weights,
+        keys,
+        target,
+        *kv_sent,
+    )
+    partial_other = swap(partial_packed)
+
+    def add_swapped(own, packed, slot):
+        return own[slot * part : (slot + 1) * part, :] + decode(packed, slot * size_part, part, head_size)[0]
+
+    def put_sums(sums, first, second, third, rows_first, rows_second):
+        sums[...] = jnp.zeros(sums.shape, f32)
+        for line, value in enumerate((first, second, third)):
+            sums[line : line + 1, :] = jnp.broadcast_to(value, (1, LANES))
+        for block in range(head_size // LANES):
+            at = slice(block * LANES, (block + 1) * LANES)
+            sums[8 + 2 * block : 9 + 2 * block, :] = rows_first[:, at]
+            sums[9 + 2 * block : 10 + 2 * block, :] = rows_second[:, at]
+
+    def get_sums(near, far):
+        count = head_size // LANES
+        sums = near[...] + far[...]
+        return (
+            sums[0:1, 0:1],
+            sums[1:2, 0:1],
+            sums[2:3, 0:1],
+            jnp.concatenate([sums[8 + 2 * b : 9 + 2 * b, :] for b in range(count)], axis=1),
+            jnp.concatenate([sums[9 + 2 * b : 10 + 2 * b, :] for b in range(count)], axis=1),
+        )
+
+    sums_shape = (8 + 2 * (head_size // LANES), LANES)
+
+    def whole_sum(value):
+        return jnp.sum(jnp.sum(value, axis=0, keepdims=True), axis=1, keepdims=True)
+
+    def sums_kernel(weight, own, packed, partial, sums):
+        found = [add_swapped(own, packed, slot) for slot in range(3)]
+        for slot in range(3):
+            partial[slot * part : (slot + 1) * part, :] = found[slot]
+        squares = jnp.sum(found[2] * found[2], axis=0, keepdims=True)
+        put_sums(
+            sums,
+            whole_sum(found[0] * found[0]),
+            whole_sum(found[1] * found[1]),
+            jnp.sum(squares, axis=1, keepdims=True),
+            squares,
+            jnp.sum(found[2] * weight[2 * part :, :], axis=0, keepdims=True),
+        )
+
+    partial, sums_own = call(
+        sums_kernel, [((3 * part, head_size), f32), (sums_shape, f32)], weights, partial_own, partial_other
+    )
+    sums = sum_z(sums_own)
+
+    def updated(weight, down_squares, partial, *sums):
+        *totals, sq_down, cross_down = get_sums(*sums)
+        found = []
+        for slot in range(3):
+            norm = jnp.sqrt(totals[slot] + 1e-06)
+            ratio = scales[slot] / norm
+            matrix = weight[slot * part : (slot + 1) * part, :]
+            grad = partial[slot * part : (slot + 1) * part, :]
+            moved = matrix - grad * ratio
+            if slot < 2:
+                old, new = row_norm(matrix), row_norm(moved)
+            else:
+                square = down_squares[...]
+                old = jnp.sqrt(square + 1e-06)
+                square = square - 2.0 * ratio * cross_down + ratio * ratio * sq_down
+                new = jnp.sqrt(jnp.maximum(square, 0.0) + 1e-06)
+            found.append((matrix, grad, moved, old, new, norm))
+        return found, cross_down - (scales[2] / found[2][5]) * sq_down
+
+    def apply_kernel(weight, down_squares, partial, near, far, query_own, cot_own, *refs):
+        count = depth - 1
+        q_refs, oc_refs, outs = refs[:count], refs[count : 2 * count], refs[2 * count :]
+        cots, packed, query_part, sent = outs[0], outs[1], outs[2], outs[3:]
+        found, _ = updated(weight, down_squares, partial, near, far)
+        renormed = [moved * (old / new) for _, _, moved, old, new, _ in found]
+        two = split(jnp.concatenate(renormed[:2], axis=0))
+        third = split(renormed[2])
+        sum_two = jnp.zeros((2 * part, head_size), f32)
+        sum_one = jnp.zeros((part, head_size), f32)
+        for slot in reversed(range(depth)):
+            if slot == 0:
+                query_rows, cot_rows = query_own[...], cot_own[...]
+            else:
+                query_rows = decode(q_refs[slot - 1], 0, tokens, head_size)[0]
+                cot_rows = decode(oc_refs[slot - 1], 0, tokens, head_size)[0]
+            query_rows, cot_rows = split(query_rows), split(cot_rows)
+            both = dot3(query_rows, two, NT)
+            h_cot = dot3(cot_rows, third, NT)
+            before, linear = both[:, :part], both[:, part:]
+            _, act, slope = silu_parts(before)
+            grads = split(jnp.concatenate([h_cot * linear * slope, h_cot * act], axis=1))
+            sum_two = sum_two + dot3(grads, query_rows, TN)
+            sum_one = sum_one + dot3(split(act * linear), cot_rows, TN)
+            query_rows = dot3(grads, two, NN)
+            if slot == 0:
+                query_part[...] = query_rows
+            else:
+                put(sent[slot - 1], 0, encode(query_rows))
+        cots[: 2 * part, :] = sum_two
+        cots[2 * part :, :] = sum_one
+        end = put(packed, 0, encode(sum_two[:part]))
+        end = put(packed, end, encode(sum_two[part:]))
+        put(packed, end, encode(sum_one))
+
+    cots_own, cots_packed, query_part, *query_slots = call(
+        apply_kernel,
+        [((3 * part, head_size), f32), ((3 * size_part, LANES), bf16), ((tokens, head_size), f32)]
+        + [((size_one, LANES), bf16)] * (depth - 1),
+        weights,
+        down_sq,
+        partial,
+        *sums,
+        queries,
+        out_cot,
+        *q_sent,
+        *oc_sent,
+    )
+    cots_other = swap(cots_packed)
+
+    def moved_grad(entry, grad, along):
+        _, _, moved, old, new, _ = entry
+        return (old / new) * (grad - moved * (along / (new * new)))
+
+    def inner_kernel(weight, down_squares, partial, near, far, own, packed, cots, inners):
+        found, _ = updated(weight, down_squares, partial, near, far)
+        totals = []
+        for slot in range(3):
+            grad = add_swapped(own, packed, slot)
+            cots[slot * part : (slot + 1) * part, :] = grad
+            if slot < 2:
+                along = jnp.sum(found[slot][2] * grad, axis=1, keepdims=True)
+                totals.append(-whole_sum(found[slot][1] * moved_grad(found[slot], grad, along)))
+        put_sums(
+            inners,
+            totals[0],
+            totals[1],
+            jnp.zeros((1, 1), f32),
+            jnp.sum(found[2][2] * grad, axis=0, keepdims=True),
+            jnp.sum(found[2][1] * grad, axis=0, keepdims=True),
+        )
+
+    cots, inners_own = call(
+        inner_kernel,
+        [((3 * part, head_size), f32), (sums_shape, f32)],
+        weights,
+        down_sq,
+        partial,
+        *sums,
+        cots_own,
+        cots_other,
+    )
+    inners = sum_z(inners_own)
+
+    def second_kernel(spot, weight, down_squares, partial, near, far, cots, inner_near, inner_far, mids, *refs):
+        key_high, key_low, target_high, target_low = refs[:4]
+        key_part, target_part, mine, other, down_part = refs[4:9]
+        sent, (whole, direct_rows) = refs[9:-2], refs[-2:]
+        found, moved_dot = updated(weight, down_squares, partial, near, far)
+        inner_gate, inner_up, _, along_down, dot_down = get_sums(inner_near, inner_far)
+        directions = []
+        for slot in range(3):
+            matrix, change, moved, old, new, norm = found[slot]
+            grad = cots[slot * part : (slot + 1) * part, :]
+            if slot < 2:
+                along = jnp.sum(moved * grad, axis=1, keepdims=True)
+                inner = (inner_gate, inner_up)[slot]
+            else:
+                along = along_down
+                inner = -jnp.sum(
+                    (old / new) * (dot_down - moved_dot * (along / (new * new))), axis=1, keepdims=True
+                )
+            back = moved_grad(found[slot], grad, along)
+            direct_rows[slot * part : (slot + 1) * part, :] = back + (along / (new * old)) * matrix
+            directions.append((scales[slot] / norm) * (-back - change * (inner / (norm * norm))))
+        turn_two = split(jnp.concatenate(directions[:2], axis=0))
+        turn_one = split(directions[2])
+        key_matrix = join(turn_two, split(weight[: 2 * part, :]), axis=0)
+        target_matrix = join(turn_one, split(weight[2 * part :, :]), axis=0)
+        sum_two = jnp.zeros((2 * part, head_size), f32)
+        sum_one = jnp.zeros((part, head_size), f32)
+        for slot in reversed(range(depth)):
+            at = slice(slot * tokens, (slot + 1) * tokens)
+            key_rows = (key_high[at, :], key_low[at, :])
+            target_rows = (target_high[at, :], target_low[at, :])
+            both = dot3(key_rows, turn_two, NT)
+            c_hidden = dot3(target_rows, turn_one, NT)
+            c_bgrad, c_lgrad = both[:, :part], both[:, part:]
+            before, linear = mids[at, :part], mids[at, part : 2 * part]
+            hgrad = mids[at, 2 * part :]
+            sigma, act, slope = silu_parts(before)
+            bend = sigma * (1.0 - sigma) * (2.0 + before * (1.0 - 2.0 * sigma))
+            c_linear = c_hidden * act + c_bgrad * hgrad * slope
+            c_hgrad = c_bgrad * linear * slope + c_lgrad * act
+            c_before = c_hidden * linear * slope + c_bgrad * hgrad * linear * bend + c_lgrad * hgrad * slope
+            through = split(jnp.concatenate([c_before, c_linear], axis=1))
+            grads = split(jnp.concatenate([hgrad * linear * slope, hgrad * act], axis=1))
+            c_hgrad = split(c_hgrad)
+            key_out = dot3(join(grads, through, axis=1), key_matrix, NN)
+            target_out = dot3(join(split(act * linear), c_hgrad, axis=1), target_matrix, NN)
+            if slot == 0:
+                key_part[...] = key_out
+                target_part[...] = target_out
+            else:
+                put(sent[slot - 1], 0, encode(key_out, target_out))
+            sum_two = sum_two + dot3(through, key_rows, TN)
+            sum_one = sum_one + dot3(c_hgrad, target_rows, TN)
+        whole[...] = sum_two
+        y = spot[1]
+        near = pl.multiple_of(y * half, half)
+        far = pl.multiple_of((1 - y) * half, half)
+        for slot in range(2):
+            rows = slice(slot * half, (slot + 1) * half)
+            mine[rows, :] = whole[pl.ds(slot * part + near, half), :] + direct_rows[pl.ds(slot * part + near, half), :]
+            other[rows, :] = whole[pl.ds(slot * part + far, half), :]
+        keep = jnp.where(y == 0, 1.0, 0.0)
+        down_part[...] = jnp.transpose(sum_one + direct_rows[2 * part :, :] * keep)
+
+    key_part, target_part, rows_mine, rows_other, down_part, *grad_slots = call(
+        second_kernel,
+        [((tokens, head_size), f32)] * 2
+        + [((2 * half, head_size), f32)] * 2
+        + [((head_size, part), f32)]
+        + [((size_two, LANES), bf16)] * (depth - 1),
+        spot,
+        weights,
+        down_sq,
+        partial,
+        *sums,
+        cots,
+        *inners,
+        mids,
+        *kv_split,
+        scratch=[pltpu.VMEM((2 * part, head_size), f32), pltpu.VMEM((3 * part, head_size), f32)],
+        smem=1,
+    )
+    grad_back = scatter_z(grad_slots)
+    rows_out = (rows_mine + swap(rows_other)).reshape(2, half, head_size)
+    share = head_size // seq_count
+    down_all = lax.all_to_all(down_part, "seq", 0, 0, tiled=True)
+    down_all = down_all.reshape(depth, 2, share, part).sum(axis=1)
+    down_out = down_all.transpose(1, 0, 2).reshape(share, hidden_size)
+
+    query_back = scatter_z(query_slots)
+
+    def query_end_kernel(own, *refs):
+        value = own[...]
+        for ref in refs[:-1]:
+            value = value + decode(ref, 0, tokens, head_size)[0]
+        refs[-1][...] = value
+
+    (query_grad,) = call(query_end_kernel, [((tokens, head_size), f32)], query_part, *query_back)
+
+    def end_kernel(rates, key_own, target_own, *refs):
+        sent, (key_out, value_out) = refs[: depth - 1], refs[depth - 1 :]
+        key_rows, target_rows = key_own[...], target_own[...]
+        for ref in sent:
+            key_more, target_more = decode(ref, 0, tokens, head_size, 2)
+            key_rows, target_rows = key_rows + key_more, target_rows + target_more
+        key_out[...] = key_rows
+        value_out[...] = -(column(rates[...]) * target_rows)
+
+    key_grad, value_grad = call(
+        end_kernel, [((tokens, head_size), f32)] * 2, rates, key_part, target_part, *grad_back
+    )
+    return (query_grad, key_grad, value_grad, rows_out[0][None], rows_out[1][None], down_out[None])
+
+
+def fits_hidden(mesh, tokens, hidden, head_size, heads):
+    seq_count = mesh.shape["seq"]
+    head_count = mesh.shape["head"]
+    depth = seq_count // 2
+    return (
+        seq_count == 2 * head_count
+        and heads == head_count
+        and depth in (2, 4, 8)
+        and tokens <= 3 * hidden
+        and tokens == seq_count * LANES
+        and hidden == depth * LANES
+        and head_size % LANES == 0
+        and head_size % (seq_count * 8) == 0
+    )
+
+
 def solution(mesh):
     placed = (
         P("seq", "head"),
@@ -167,17 +709,22 @@
         P("head", "seq"),
         P("seq", "head"),
     )
-    return jax.shard_map(
-        body,
-        mesh=mesh,
-        in_specs=placed,
-        out_specs=(
-            P("seq", "head"),
-            P("seq", "head"),
-            P("seq", "head"),
-            P("head", "seq", None),
-            P("head", "seq", None),
-            P("head", "seq", None),
-        ),
-        check_vma=False,
-    )
+    outs = (
+        P("seq", "head"),
+        P("seq", "head"),
+        P("seq", "head"),
+        P("head", "seq", None),
+        P("head", "seq", None),
+        P("head", "seq", None),
+    )
+
+    def whole(*arrays):
+        hidden, head_size = arrays[4].shape[1:]
+        small = fits_hidden(mesh, arrays[0].shape[0], hidden, head_size, arrays[4].shape[0])
+        if not small:
+            return jax.shard_map(body, mesh=mesh, in_specs=placed, out_specs=outs, check_vma=False)(*arrays)
+
+        step = jax.shard_map(body_hidden, mesh=mesh, in_specs=placed, out_specs=outs, check_vma=False)
+        return step(*arrays)
+
+    return whole

time: 573 us -> 193 us (0.34)
  waiting for transfers between devices: 454 us -> 82.8 us
  matrix products: 64.1 us -> 0 us
  starting transfers between devices: 0.95 us -> 47.9 us
  Pallas kernels: 0 us -> 44.9 us
  other arithmetic: 30 us -> 2.34 us
  between operations: 20 us -> 0.92 us
  local copies, waits for them, and re-layouts: 3.76 us -> 11.1 us
    psum x2 -> x0, waiting for transfers between devices: 288 us -> none  [the longest x1 160 us: body(): totals = lax.psum((partials[0], partials[1], partials[2]), 'seq')]
    reduce_scatter x3 -> x0, waiting for transfers between devices: 164 us -> none  [the longest x1 64.8 us: body(): lax.psum_scatter(through_up, 'seq', scatter_dimension=1, tiled=True)]
    ppermute x0 -> x30, waiting for transfers between devices: none -> 82.7 us  [the longest x18 48.3 us: turn(): return lax.ppermute(array, 'seq', perm)]
    dot_general x27 -> x0, matrix products: 64.1 us -> none  [the longest x26 59.9 us: matmul(): jnp.dot(left, right, precision=lax.Precision.HIGHEST, preferred_element_t...]
    pallas_call x0 -> x11, Pallas kernels: none -> 44.9 us  [call(): pl.pallas_call(kernel, out_shape=[jax.ShapeDtypeStruct(shape, dtype) for...]
    ppermute x0 -> x30, starting transfers between devices: none -> 43.6 us  [the longest x18 34.6 us: turn(): return lax.ppermute(array, 'seq', perm)]
    reduce_sum x11 -> x1, other arithmetic: 24.8 us -> 0.02 us  [body_hidden(): down_all = down_all.reshape(depth, 2, share, part).sum(axis=1)]
  transfers between devices with their start and end apart: 7 -> 31, of which waited for: 5 -> 11; matrix products, arithmetic and copies ran while one was open for 8% -> 2% of each run, Pallas kernels for 0% -> 12%
where the time goes in v1:
time: 193 us; the launch traced here: 190 us
  waiting for transfers between devices  82.8 us (43%)
  starting transfers between devices  47.9 us (25%)
  Pallas kernels  44.9 us (23%)
  local copies, waits for them, and re-layouts  11.1 us (6%)
  other arithmetic  2.34 us (1%)
    ppermute x18, waiting for transfers between devices, turn(): return lax.ppermute(array, 'seq', perm)  48.3 us
    pallas_call x11, Pallas kernels, call(): pl.pallas_call(kernel, out_shape=[jax.ShapeDtypeStruct(shape, dtype) for...  44.9 us
    ppermute x18, starting transfers between devices, turn(): return lax.ppermute(array, 'seq', perm)  34.6 us
    ppermute x4, waiting for transfers between devices, sum_z(): lax.ppermute(array, 'seq', [(s, s ^ 2 * reach) for s in range(seq_count)])  14.8 us
    ppermute x3, waiting for transfers between devices, body_hidden(): lax.ppermute(og_mine, 'head', [(h, (h + step) % heads) for h in range(hea...  11 us
    ppermute x4, waiting for transfers between devices, swap(): return lax.ppermute(array, 'seq', [(s, s ^ 1) for s in range(seq_count)])  8.61 us
    unnamed x76, local copies, waits for them, and re-layouts  7.42 us
    all_to_all x1, starting transfers between devices, body_hidden(): down_all = lax.all_to_all(down_part, 'seq', 0, 0, tiled=True)  4.35 us
  transfers between devices with their start and end apart: 31, of which 11 were waited for; matrix products, arithmetic and copies ran while one was open for 2% of the time, Pallas kernels for 12%

profile of v1, /device:TPU:0, one launch (start us, length us, event | category | flops | bytes accessed | tf_op | source)
XLA Modules:
  0.0 190.0 jit_solution(3914762384829467385)
XLA Ops:
  0.6 2.2 %shard_map.137 = (f32[128,512]{1,0:T(8,128)}, bf16[1040,128]{1,0:T(8,128)(2,1)}) custom-call(f32[128,512]{1,0:T(8,128)} %key_own.1, f32[128,512]{1,0:T(8,128)} %values.1, f32[1,128]{1,0:T(1,128)} %rates.3), custom_call_target="tpu_custom_call" | custom-call | tf_op jit(solution)/shard_map/pallas_call | solution.py:245
  2.8 5.1 %collective-permute-start.2 = (bf16[1040,128]{1,0:T(8,128)(2,1)}, bf16[1040,128]{1,0:T(8,128)(2,1)S(1)}, u32[]{:S(2)}, u32[]{:S(2)}) collective-permute-start(bf16[1040,128]{1,0:T(8,128)(2,1)} %get-tuple-element.45), channel_id=1, source_target_pairs={{0,24},{4,28},{8,0},{12,4},{16,8},{20,12},{24,16},{28,20},{1,25},{... | collective-permute-start | bytes 798728 | tf_op jit(solution)/shard_map/ppermute | solution.py:288
  15.2 22.3 %collective-permute-done.1.refs_1_ = bf16[1040,128]{1,0:T(8,128)(2,1)S(1)} collective-permute-done((bf16[1040,128]{1,0:T(8,128)(2,1)}, bf16[1040,128]{1,0:T(8,128)(2,1)S(1)}, u32[]{:S(2)}, u32[]{:S(2)}) %collective-permute-start.1) | collective-permute-done | bytes 266272 | tf_op jit(solution)/shard_map/ppermute | solution.py:288
  38.4 6.7 %shard_map.138 = (bf16[512,512]{1,0:T(8,128)(2,1)}, bf16[512,512]{1,0:T(8,128)(2,1)}, bf16[512,512]{1,0:T(8,128)(2,1)}, bf16[512,512]{1,0:T(8,128)(2,1)}, f32[51...) custom-call(f32[384,512]{1,0:T(8,128)} %pad_maximum_fusion.weight, f32[128,512]{1,0:T(8,128)} %key_own.1, ...), custom_call_target="tpu_custom_call" | custom-call | tf_op jit(solution)/shard_map/pallas_call | solution.py:245
  47.7 5.6 %collective-permute-done.10.refs_3_ = bf16[128,1024]{1,0:T(8,128)(2,1)S(1)} collective-permute-done((bf16[128,1024]{1,0:T(8,128)(2,1)S(1)}, bf16[128,1024]{1,0:T(8,128)(2,1)S(1)}, u32[]{:S(2)}, u32[]{:S(2)}) %collective-permute-start.10) | collective-permute-done | bytes 262176 | tf_op jit(solution)/shard_map/ppermute | solution.py:321
  53.3 5.4 %collective-permute-done.9.refs_2_ = bf16[128,1024]{1,0:T(8,128)(2,1)S(1)} collective-permute-done((bf16[128,1024]{1,0:T(8,128)(2,1)S(1)}, bf16[128,1024]{1,0:T(8,128)(2,1)S(1)}, u32[]{:S(2)}, u32[]{:S(2)}) %collective-permute-start.9) | collective-permute-done | bytes 262176 | tf_op jit(solution)/shard_map/ppermute | solution.py:321
  60.4 4.1 %shard_map.140 = (f32[128,512]{1,0:T(8,128)}, bf16[528,128]{1,0:T(8,128)(2,1)}, bf16[528,128]{1,0:T(8,128)(2,1)}, bf16[528,128]{1,0:T(8,128)(2,1)}) custom-call(s32[3]{0:T(128)} %pad_add_fusion.spot, bf16[512,512]{1,0:T(8,128)(2,1)} %mine.1, bf16[512,512]{1,0:T(8,128)(2,1)} %copy-done.1, bf16[128,1024]{1,0:T(8,128)(2,1)} %copy-done.10, ...), custom_call_target="tpu_custom_call" | custom-call | tf_op jit(solution)/shard_map/pallas_call | solution.py:245
  64.7 4.1 %collective-permute-start.12 = (bf16[528,128]{1,0:T(8,128)(2,1)}, bf16[528,128]{1,0:T(8,128)(2,1)S(1)}, u32[]{:S(2)}, u32[]{:S(2)}) collective-permute-start(bf16[528,128]{1,0:T(8,128)(2,1)} %get-tuple-element.52), channel_id=1, source_target_pairs={{0,16},{4,20},{8,24},{12,28},{16,0},{20,4},{24,8},{28,12},{1,17},{... | collective-permute-start | bytes 405512 | tf_op jit(solution)/shard_map/ppermute | solution.py:288
  68.8 2.0 %collective-permute-start.13 = (bf16[528,128]{1,0:T(8,128)(2,1)}, bf16[528,128]{1,0:T(8,128)(2,1)S(1)}, u32[]{:S(2)}, u32[]{:S(2)}) collective-permute-start(bf16[528,128]{1,0:T(8,128)(2,1)} %get-tuple-element.53), channel_id=1, source_target_pairs={{0,8},{4,12},{8,16},{12,20},{16,24},{20,28},{24,0},{28,4},{1,9},{5... | collective-permute-start | bytes 405512 | tf_op jit(solution)/shard_map/ppermute | solution.py:288
  70.8 2.2 %shard_map.136 = (bf16[528,128]{1,0:T(8,128)(2,1)}, f32[1,512]{1,0:T(1,128)}) custom-call(f32[128,512]{1,0:T(8,128)} %query_own.1, f32[512,512]{1,0:T(8,128)} %bitcast.19), custom_call_target="tpu_custom_call" | custom-call | tf_op jit(solution)/shard_map/pallas_call | solution.py:245
  73.0 1.8 collective-permute-start.16
  75.6 2.8 %shard_map.139 = (f32[384,512]{1,0:T(8,128)}, f32[16,128]{1,0:T(8,128)}) custom-call(f32[384,512]{1,0:T(8,128)} %pad_maximum_fusion.weight, f32[384,512]{1,0:T(8,128)} %get-tuple-element.46.own, bf16[1584,128]{1,0:T(8,128)(2,1)} %copy-done.3), custom_call_target="tpu_custom_call" | custom-call | tf_op jit(solution)/shard_map/pallas_call | solution.py:245
  78.7 7.4 %collective-permute-done.12.refs_1_ = bf16[528,128]{1,0:T(8,128)(2,1)S(1)} collective-permute-done((bf16[528,128]{1,0:T(8,128)(2,1)}, bf16[528,128]{1,0:T(8,128)(2,1)S(1)}, u32[]{:S(2)}, u32[]{:S(2)}) %collective-permute-start.12) | collective-permute-done | bytes 135200 | tf_op jit(solution)/shard_map/ppermute | solution.py:288
  86.8 2.3 %shard_map.141 = (f32[128,512]{1,0:T(8,128)}, bf16[528,128]{1,0:T(8,128)(2,1)}) custom-call(f32[128,512]{1,0:T(8,128)} %get-tuple-element.50.own, bf16[528,128]{1,0:T(8,128)(2,1)} %copy-done.24, bf16[528,128]{1,0:T(8,128)(2,1)} %copy-done.25, bf16[528,128]{1,0:T(8,128)(2,1)} %copy-done.26), custom_call_target="tpu_custom_call" | custom-call | tf_op jit(solution)/shard_map/pallas_call | solution.py:245
  89.1 3.8 %collective-permute-start.19 = (bf16[528,128]{1,0:T(8,128)(2,1)}, bf16[528,128]{1,0:T(8,128)(2,1)S(1)}, u32[]{:S(2)}, u32[]{:S(2)}) collective-permute-start(bf16[528,128]{1,0:T(8,128)(2,1)} %get-tuple-element.56), channel_id=1, source_target_pairs={{0,24},{4,28},{8,0},{12,4},{16,8},{20,12},{24,16},{28,20},{1,25},{... | collective-permute-start | bytes 405512 | tf_op jit(solution)/shard_map/ppermute | solution.py:288
  93.5 2.4 %collective-permute-start.5 = (f32[16,128]{1,0:T(8,128)S(1)}, f32[16,128]{1,0:T(8,128)S(1)}, u32[]{:S(2)}, u32[]{:S(2)}) collective-permute-start(f32[16,128]{1,0:T(8,128)S(1)} %add.20.near), channel_id=1, source_target_pairs={{0,16},{4,20},{8,24},{12,28},{16,0},{20,4},{24,8},{28,12},{1,17},{... | collective-permute-start | bytes 24584 | tf_op jit(solution)/shard_map/ppermute | solution.py:302
  95.9 6.6 %collective-permute-done.5.far = f32[16,128]{1,0:T(8,128)S(1)} collective-permute-done((f32[16,128]{1,0:T(8,128)S(1)}, f32[16,128]{1,0:T(8,128)S(1)}, u32[]{:S(2)}, u32[]{:S(2)}) %collective-permute-start.5) | collective-permute-done | bytes 8224 | tf_op jit(solution)/shard_map/ppermute | solution.py:302
  103.3 7.5 %shard_map.142 = (f32[384,512]{1,0:T(8,128)}, bf16[1584,128]{1,0:T(8,128)(2,1)}, f32[128,512]{1,0:T(8,128)}, bf16[528,128]{1,0:T(8,128)(2,1)}, bf16[528,128]{1,0:T(8,128)(2,1)}, /*index=5*/bf16[528,128]{1,0:T(8,128)(2,1)}) custom-call(f32[384,512]{1,0:T(8,128)} %pad_maximum_fusion.weight, f32[1,512]{1,0:T(1,128)} %get-tuple-element.43.down_squares, ...), custom_call_target="tpu_custom_call" | custom-call | tf_op jit(solution)/shard_map/pallas_call | solution.py:245
  111.4 8.6 %collective-permute-done.23.packed = bf16[1584,128]{1,0:T(8,128)(2,1)S(1)} collective-permute-done((bf16[1584,128]{1,0:T(8,128)(2,1)}, bf16[1584,128]{1,0:T(8,128)(2,1)S(1)}, u32[]{:S(2)}, u32[]{:S(2)}) %collective-permute-start.23) | collective-permute-done | bytes 405536 | tf_op jit(solution)/shard_map/ppermute | solution.py:291
  120.8 3.5 %shard_map.144 = (f32[384,512]{1,0:T(8,128)}, f32[16,128]{1,0:T(8,128)}) custom-call(f32[384,512]{1,0:T(8,128)} %pad_maximum_fusion.weight, f32[1,512]{1,0:T(1,128)} %get-tuple-element.43.down_squares, f32[384,512]{1,0:T(8,128)} %get-tuple-element.48.partial, f32[16,128]{1,0:T(8,128)} %copy-done.27, f32[16,128]{1,0:T(8,128)} %copy-done.28, ...), custom_call_target="tpu_custom_call" | custom-call | tf_op jit(solution)/shard_map/pallas_call | solution.py:245
  124.3 3.9 %collective-permute-done.24 = f32[16,128]{1,0:T(8,128)S(1)} collective-permute-done((f32[16,128]{1,0:T(8,128)}, f32[16,128]{1,0:T(8,128)S(1)}, u32[]{:S(2)}, u32[]{:S(2)}) %collective-permute-start.24) | collective-permute-done | bytes 8224 | tf_op jit(solution)/shard_map/ppermute | solution.py:302
  129.2 4.3 %collective-permute-done.25.inner_far = f32[16,128]{1,0:T(8,128)S(1)} collective-permute-done((f32[16,128]{1,0:T(8,128)S(1)}, f32[16,128]{1,0:T(8,128)S(1)}, u32[]{:S(2)}, u32[]{:S(2)}) %collective-permute-start.25) | collective-permute-done | bytes 8224 | tf_op jit(solution)/shard_map/ppermute | solution.py:302
  134.1 8.9 %shard_map.145 = (f32[128,512]{1,0:T(8,128)}, f32[128,512]{1,0:T(8,128)}, f32[128,512]{1,0:T(8,128)}, f32[128,512]{1,0:T(8,128)}, f32[512,128]{1,0:T(8,128)}, /*...) custom-call(s32[3]{0:T(128)} %pad_add_fusion.spot, ...), custom_call_target="tpu_custom_call" | custom-call | tf_op jit(solution)/shard_map/pallas_call | solution.py:245
  143.2 4.3 %all-to-all-start = ((f32[8,64,128]{2,1,0:T(8,128)}), f32[8,64,128]{2,1,0:T(8,128)S(1)}, u32[]{:S(2)}, u32[]{:S(2)}) async-start(f32[8,64,128]{2,1,0:T(8,128)} %bitcast.22), calls=%async_computation | async-start | bytes 524288 | tf_op jit(solution)/shard_map/all_to_all | solution.py:655
  147.6 3.8 %collective-permute-start.20 = (bf16[528,128]{1,0:T(8,128)(2,1)S(1)}, bf16[528,128]{1,0:T(8,128)(2,1)S(1)}, u32[]{:S(2)}, u32[]{:S(2)}) collective-permute-start(bf16[528,128]{1,0:T(8,128)(2,1)S(1)} %copy-done.36), channel_id=1, source_target_pairs={{0,24},{4,28},{8,0},{12,4},{16,8},{20,12},{24,16},{28,20},{1,25},{... | collective-permute-start | bytes 405512 | tf_op jit(solution)/shard_map/ppermute | solution.py:288
  152.5 2.8 %collective-permute-start.26 = (bf16[1040,128]{1,0:T(8,128)(2,1)}, bf16[1040,128]{1,0:T(8,128)(2,1)S(1)}, u32[]{:S(2)}, u32[]{:S(2)}) collective-permute-start(bf16[1040,128]{1,0:T(8,128)(2,1)} %get-tuple-element.72), channel_id=1, source_target_pairs={{0,24},{4,28},{8,0},{12,4},{16,8},{20,12},{24,16},{28,20},{1,25},{... | collective-permute-start | bytes 798728 | tf_op jit(solution)/shard_map/ppermute | solution.py:288
  155.3 3.1 %collective-permute-done.20.refs_0_ = bf16[528,128]{1,0:T(8,128)(2,1)S(1)} collective-permute-done((bf16[528,128]{1,0:T(8,128)(2,1)S(1)}, bf16[528,128]{1,0:T(8,128)(2,1)S(1)}, u32[]{:S(2)}, u32[]{:S(2)}) %collective-permute-start.20) | collective-permute-done | bytes 135200 | tf_op jit(solution)/shard_map/ppermute | solution.py:288
  158.4 8.2 %collective-permute-start.27 = (bf16[1040,128]{1,0:T(8,128)(2,1)S(1)}, bf16[1040,128]{1,0:T(8,128)(2,1)S(1)}, u32[]{:S(2)}, u32[]{:S(2)}) collective-permute-start(bf16[1040,128]{1,0:T(8,128)(2,1)S(1)} %copy-done.33), channel_id=1, source_target_pairs={{0,16},{4,20},{8,24},{12,28},{16,0},{20,4},{24,8},{28,12},{1,17},{... | collective-permute-start | bytes 798728 | tf_op jit(solution)/shard_map/ppermute | solution.py:288
  166.6 5.0 %collective-permute-done.21.refs_1_ = bf16[528,128]{1,0:T(8,128)(2,1)S(1)} collective-permute-done((bf16[528,128]{1,0:T(8,128)(2,1)S(1)}, bf16[528,128]{1,0:T(8,128)(2,1)S(1)}, u32[]{:S(2)}, u32[]{:S(2)}) %collective-permute-start.21) | collective-permute-done | bytes 135200 | tf_op jit(solution)/shard_map/ppermute | solution.py:288
  172.4 2.2 %shard_map.143 = f32[128,512]{1,0:T(8,128)} custom-call(f32[128,512]{1,0:T(8,128)} %get-tuple-element.57.own, bf16[528,128]{1,0:T(8,128)(2,1)} %copy-done.21, bf16[528,128]{1,0:T(8,128)(2,1)} %copy-done.22, bf16[528,128]{1,0:T(8,128)(2,1)} %copy-done.23), custom_call_target="tpu_custom_call" | custom-call | tf_op jit(solution)/shard_map/pallas_call | solution.py:245
  175.3 10.3 %collective-permute-done.27.refs_1_ = bf16[1040,128]{1,0:T(8,128)(2,1)S(1)} collective-permute-done((bf16[1040,128]{1,0:T(8,128)(2,1)S(1)}, bf16[1040,128]{1,0:T(8,128)(2,1)S(1)}, u32[]{:S(2)}, u32[]{:S(2)}) %collective-permute-start.27) | collective-permute-done | bytes 266272 | tf_op jit(solution)/shard_map/ppermute | solution.py:288
  186.5 2.6 %shard_map.146 = (f32[128,512]{1,0:T(8,128)}, f32[128,512]{1,0:T(8,128)}) custom-call(f32[1,128]{1,0:T(1,128)} %rates.3, f32[128,512]{1,0:T(8,128)} %get-tuple-element.70.key_own, f32[128,512]{1,0:T(8,128)} %get-tuple-element.71.target_own, bf16[1040,128]{1,0:T(8,128)(2,1)} %copy-done.4, bf16[1040,128]{1,0:T(8,128)(2,1)} %copy-done.5, ...), custom_call_target="tpu_custom_call" | custom-call | tf_op jit(solution)/shard_map/pallas_call | solution.py:245
  (129 shorter events, 23.1 us)
Async XLA Ops:
  2.8 12.4 %collective-permute-start.2 = (bf16[1040,128]{1,0:T(8,128)(2,1)}, bf16[1040,128]{1,0:T(8,128)(2,1)S(1)}, u32[]{:S(2)}, u32[]{:S(2)}) collective-permute-start(bf16[1040,128]{1,0:T(8,128)(2,1)} %get-tuple-element.45), channel_id=1, source_target_pairs={{0,24},{4,28},{8,0},{12,4},{16,8},{20,12},{24,16},{28,20},{1,25},{... | collective-permute-start | bytes 798728 | tf_op jit(solution)/shard_map/ppermute | solution.py:288
  7.9 29.6 %collective-permute-start.1 = (bf16[1040,128]{1,0:T(8,128)(2,1)}, bf16[1040,128]{1,0:T(8,128)(2,1)S(1)}, u32[]{:S(2)}, u32[]{:S(2)}) collective-permute-start(bf16[1040,128]{1,0:T(8,128)(2,1)} %get-tuple-element.45), channel_id=1, source_target_pairs={{0,16},{4,20},{8,24},{12,28},{16,0},{20,4},{24,8},{28,12},{1,17},{... | collective-permute-start | bytes 798728 | tf_op jit(solution)/shard_map/ppermute | solution.py:288
  7.9 29.6 %collective-permute-start = (bf16[1040,128]{1,0:T(8,128)(2,1)}, bf16[1040,128]{1,0:T(8,128)(2,1)S(1)}, u32[]{:S(2)}, u32[]{:S(2)}) collective-permute-start(bf16[1040,128]{1,0:T(8,128)(2,1)} %get-tuple-element.45), channel_id=1, source_target_pairs={{0,8},{4,12},{8,16},{12,20},{16,24},{20,28},{24,0},{28,4},{1,9},{5... | collective-permute-start | bytes 798728 | tf_op jit(solution)/shard_map/ppermute | solution.py:288
  8.9 37.7 %collective-permute-start.7 = (bf16[128,1024]{1,0:T(8,128)(2,1)}, bf16[128,1024]{1,0:T(8,128)(2,1)S(1)}, u32[]{:S(2)}, u32[]{:S(2)}) collective-permute-start(bf16[128,1024]{1,0:T(8,128)(2,1)} %param.17), channel_id=1, source_target_pairs={{0,0},{1,8},{2,16},{3,24},{4,4},{5,12},{6,20},{7,28},{8,2},{9,10},... | collective-permute-start | bytes 786440 | tf_op jit(solution)/shard_map/ppermute | solution.py:318
  10.5 48.3 %collective-permute-start.6 = (bf16[512,512]{1,0:T(8,128)(2,1)S(1)}, bf16[512,512]{1,0:T(8,128)(2,1)S(1)}, u32[]{:S(2)}, u32[]{:S(2)}) collective-permute-start(bf16[512,512]{1,0:T(8,128)(2,1)S(1)} %copy-done), channel_id=1, source_target_pairs={{0,4},{4,0},{8,12},{12,8},{16,20},{20,16},{24,28},{28,24},{1,5},{5... | collective-permute-start | bytes 1572872 | tf_op jit(solution)/shard_map/ppermute | solution.py:291
  45.1 29.7 %collective-permute-start.3 = (bf16[1584,128]{1,0:T(8,128)(2,1)}, bf16[1584,128]{1,0:T(8,128)(2,1)S(1)}, u32[]{:S(2)}, u32[]{:S(2)}) collective-permute-start(bf16[1584,128]{1,0:T(8,128)(2,1)} %get-tuple-element.47), channel_id=1, source_target_pairs={{0,4},{4,0},{8,12},{12,8},{16,20},{20,16},{24,28},{28,24},{1,5},{5... | collective-permute-start | bytes 1216520 | tf_op jit(solution)/shard_map/ppermute | solution.py:291
  46.6 6.7 %collective-permute-start.10 = (bf16[128,1024]{1,0:T(8,128)(2,1)S(1)}, bf16[128,1024]{1,0:T(8,128)(2,1)S(1)}, u32[]{:S(2)}, u32[]{:S(2)}) collective-permute-start(bf16[128,1024]{1,0:T(8,128)(2,1)S(1)} %collective-permute-done.7.refs_0_), channel_id=1, source_target_pairs={{0,3},{1,0},{2,1},{3,2},{4,7},{5,4},{6,5},{7,6},{8,11},{9,8},{10,9... | collective-permute-start | bytes 786440 | tf_op jit(solution)/shard_map/ppermute | solution.py:321
  46.6 12.1 %collective-permute-start.9 = (bf16[128,1024]{1,0:T(8,128)(2,1)S(1)}, bf16[128,1024]{1,0:T(8,128)(2,1)S(1)}, u32[]{:S(2)}, u32[]{:S(2)}) collective-permute-start(bf16[128,1024]{1,0:T(8,128)(2,1)S(1)} %collective-permute-done.7.refs_0_), channel_id=1, source_target_pairs={{0,2},{1,3},{2,0},{3,1},{4,6},{5,7},{6,4},{7,5},{8,10},{9,11},{10,... | collective-permute-start | bytes 786440 | tf_op jit(solution)/shard_map/ppermute | solution.py:321
  46.7 12.1 %collective-permute-start.8 = (bf16[128,1024]{1,0:T(8,128)(2,1)S(1)}, bf16[128,1024]{1,0:T(8,128)(2,1)S(1)}, u32[]{:S(2)}, u32[]{:S(2)}) collective-permute-start(bf16[128,1024]{1,0:T(8,128)(2,1)S(1)} %collective-permute-done.7.refs_0_), channel_id=1, source_target_pairs={{0,1},{1,2},{2,3},{3,0},{4,5},{5,6},{6,7},{7,4},{8,9},{9,10},{10,1... | collective-permute-start | bytes 786440 | tf_op jit(solution)/shard_map/ppermute | solution.py:321
  64.4 14.0 %collective-permute-start.11 = (bf16[528,128]{1,0:T(8,128)(2,1)}, bf16[528,128]{1,0:T(8,128)(2,1)S(1)}, u32[]{:S(2)}, u32[]{:S(2)}) collective-permute-start(bf16[528,128]{1,0:T(8,128)(2,1)} %get-tuple-element.51), channel_id=1, source_target_pairs={{0,24},{4,28},{8,0},{12,4},{16,8},{20,12},{24,16},{28,20},{1,25},{... | collective-permute-start | bytes 405512 | tf_op jit(solution)/shard_map/ppermute | solution.py:288
  64.7 21.4 %collective-permute-start.12 = (bf16[528,128]{1,0:T(8,128)(2,1)}, bf16[528,128]{1,0:T(8,128)(2,1)S(1)}, u32[]{:S(2)}, u32[]{:S(2)}) collective-permute-start(bf16[528,128]{1,0:T(8,128)(2,1)} %get-tuple-element.52), channel_id=1, source_target_pairs={{0,16},{4,20},{8,24},{12,28},{16,0},{20,4},{24,8},{28,12},{1,17},{... | collective-permute-start | bytes 405512 | tf_op jit(solution)/shard_map/ppermute | solution.py:288
  68.8 17.3 %collective-permute-start.13 = (bf16[528,128]{1,0:T(8,128)(2,1)}, bf16[528,128]{1,0:T(8,128)(2,1)S(1)}, u32[]{:S(2)}, u32[]{:S(2)}) collective-permute-start(bf16[528,128]{1,0:T(8,128)(2,1)} %get-tuple-element.53), channel_id=1, source_target_pairs={{0,8},{4,12},{8,16},{12,20},{16,24},{20,28},{24,0},{28,4},{1,9},{5... | collective-permute-start | bytes 405512 | tf_op jit(solution)/shard_map/ppermute | solution.py:288
  73.0 19.9 %collective-permute-start.16 = (bf16[528,128]{1,0:T(8,128)(2,1)}, bf16[528,128]{1,0:T(8,128)(2,1)S(1)}, u32[]{:S(2)}, u32[]{:S(2)}) collective-permute-start(bf16[528,128]{1,0:T(8,128)(2,1)} %get-tuple-element.55), channel_id=1, source_target_pairs={{0,24},{4,28},{8,0},{12,4},{16,8},{20,12},{24,16},{28,20},{1,25},{... | collective-permute-start | bytes 405512 | tf_op jit(solution)/shard_map/ppermute | solution.py:288
  74.8 18.7 %collective-permute-start.15 = (bf16[528,128]{1,0:T(8,128)(2,1)}, bf16[528,128]{1,0:T(8,128)(2,1)S(1)}, u32[]{:S(2)}, u32[]{:S(2)}) collective-permute-start(bf16[528,128]{1,0:T(8,128)(2,1)} %get-tuple-element.55), channel_id=1, source_target_pairs={{0,16},{4,20},{8,24},{12,28},{16,0},{20,4},{24,8},{28,12},{1,17},{... | collective-permute-start | bytes 405512 | tf_op jit(solution)/shard_map/ppermute | solution.py:288
  78.4 14.5 %collective-permute-start.4 = (f32[16,128]{1,0:T(8,128)}, f32[16,128]{1,0:T(8,128)S(1)}, u32[]{:S(2)}, u32[]{:S(2)}) collective-permute-start(f32[16,128]{1,0:T(8,128)} %get-tuple-element.49), channel_id=1, source_target_pairs={{0,8},{4,12},{8,0},{12,4},{16,24},{20,28},{24,16},{28,20},{1,9},{5... | collective-permute-start | bytes 24584 | tf_op jit(solution)/shard_map/ppermute | solution.py:302
  86.1 9.8 %collective-permute-start.14 = (bf16[528,128]{1,0:T(8,128)(2,1)S(1)}, bf16[528,128]{1,0:T(8,128)(2,1)S(1)}, u32[]{:S(2)}, u32[]{:S(2)}) collective-permute-start(bf16[528,128]{1,0:T(8,128)(2,1)S(1)} %copy-done.37), channel_id=1, source_target_pairs={{0,8},{4,12},{8,16},{12,20},{16,24},{20,28},{24,0},{28,4},{1,9},{5... | collective-permute-start | bytes 405512 | tf_op jit(solution)/shard_map/ppermute | solution.py:288
  89.1 13.5 %collective-permute-start.19 = (bf16[528,128]{1,0:T(8,128)(2,1)}, bf16[528,128]{1,0:T(8,128)(2,1)S(1)}, u32[]{:S(2)}, u32[]{:S(2)}) collective-permute-start(bf16[528,128]{1,0:T(8,128)(2,1)} %get-tuple-element.56), channel_id=1, source_target_pairs={{0,24},{4,28},{8,0},{12,4},{16,8},{20,12},{24,16},{28,20},{1,25},{... | collective-permute-start | bytes 405512 | tf_op jit(solution)/shard_map/ppermute | solution.py:288
  92.9 9.7 %collective-permute-start.18 = (bf16[528,128]{1,0:T(8,128)(2,1)}, bf16[528,128]{1,0:T(8,128)(2,1)S(1)}, u32[]{:S(2)}, u32[]{:S(2)}) collective-permute-start(bf16[528,128]{1,0:T(8,128)(2,1)} %get-tuple-element.56), channel_id=1, source_target_pairs={{0,16},{4,20},{8,24},{12,28},{16,0},{20,4},{24,8},{28,12},{1,17},{... | collective-permute-start | bytes 405512 | tf_op jit(solution)/shard_map/ppermute | solution.py:288
  92.9 9.7 %collective-permute-start.17 = (bf16[528,128]{1,0:T(8,128)(2,1)}, bf16[528,128]{1,0:T(8,128)(2,1)S(1)}, u32[]{:S(2)}, u32[]{:S(2)}) collective-permute-start(bf16[528,128]{1,0:T(8,128)(2,1)} %get-tuple-element.56), channel_id=1, source_target_pairs={{0,8},{4,12},{8,16},{12,20},{16,24},{20,28},{24,0},{28,4},{1,9},{5... | collective-permute-start | bytes 405512 | tf_op jit(solution)/shard_map/ppermute | solution.py:288
  93.5 9.0 %collective-permute-start.5 = (f32[16,128]{1,0:T(8,128)S(1)}, f32[16,128]{1,0:T(8,128)S(1)}, u32[]{:S(2)}, u32[]{:S(2)}) collective-permute-start(f32[16,128]{1,0:T(8,128)S(1)} %add.20.near), channel_id=1, source_target_pairs={{0,16},{4,20},{8,24},{12,28},{16,0},{20,4},{24,8},{28,12},{1,17},{... | collective-permute-start | bytes 24584 | tf_op jit(solution)/shard_map/ppermute | solution.py:302
  110.8 9.2 %collective-permute-start.23 = (bf16[1584,128]{1,0:T(8,128)(2,1)}, bf16[1584,128]{1,0:T(8,128)(2,1)S(1)}, u32[]{:S(2)}, u32[]{:S(2)}) collective-permute-start(bf16[1584,128]{1,0:T(8,128)(2,1)} %get-tuple-element.62), channel_id=1, source_target_pairs={{0,4},{4,0},{8,12},{12,8},{16,20},{20,16},{24,28},{28,24},{1,5},{5... | collective-permute-start | bytes 1216520 | tf_op jit(solution)/shard_map/ppermute | solution.py:291
  124.3 3.9 %collective-permute-start.24 = (f32[16,128]{1,0:T(8,128)}, f32[16,128]{1,0:T(8,128)S(1)}, u32[]{:S(2)}, u32[]{:S(2)}) collective-permute-start(f32[16,128]{1,0:T(8,128)} %get-tuple-element.64), channel_id=1, source_target_pairs={{0,8},{4,12},{8,0},{12,4},{16,24},{20,28},{24,16},{28,20},{1,9},{5... | collective-permute-start | bytes 24584 | tf_op jit(solution)/shard_map/ppermute | solution.py:302
  128.9 4.5 %collective-permute-start.25 = (f32[16,128]{1,0:T(8,128)S(1)}, f32[16,128]{1,0:T(8,128)S(1)}, u32[]{:S(2)}, u32[]{:S(2)}) collective-permute-start(f32[16,128]{1,0:T(8,128)S(1)} %add.22.inner_near), channel_id=1, source_target_pairs={{0,16},{4,20},{8,24},{12,28},{16,0},{20,4},{24,8},{28,12},{1,17},{... | collective-permute-start | bytes 24584 | tf_op jit(solution)/shard_map/ppermute | solution.py:302
  142.9 31.6 %collective-permute-start.29 = (f32[128,512]{1,0:T(8,128)}, f32[128,512]{1,0:T(8,128)S(1)}, u32[]{:S(2)}, u32[]{:S(2)}) collective-permute-start(f32[128,512]{1,0:T(8,128)} %get-tuple-element.78), channel_id=1, source_target_pairs={{0,4},{4,0},{8,12},{12,8},{16,20},{20,16},{24,28},{28,24},{1,5},{5... | collective-permute-start | bytes 786440 | tf_op jit(solution)/shard_map/ppermute | solution.py:291
  143.2 28.4 %copy-start.32 = (bf16[1040,128]{1,0:T(8,128)(2,1)S(1)}, bf16[1040,128]{1,0:T(8,128)(2,1)}, u32[]{:S(2)}) copy-start(bf16[1040,128]{1,0:T(8,128)(2,1)} %get-tuple-element.74) | copy-start | bytes 798724
  143.2 45.9 %all-to-all-start = ((f32[8,64,128]{2,1,0:T(8,128)}), f32[8,64,128]{2,1,0:T(8,128)S(1)}, u32[]{:S(2)}, u32[]{:S(2)}) async-start(f32[8,64,128]{2,1,0:T(8,128)} %bitcast.22), calls=%async_computation | async-start | bytes 524288 | tf_op jit(solution)/shard_map/all_to_all | solution.py:655
  147.6 10.9 %collective-permute-start.20 = (bf16[528,128]{1,0:T(8,128)(2,1)S(1)}, bf16[528,128]{1,0:T(8,128)(2,1)S(1)}, u32[]{:S(2)}, u32[]{:S(2)}) collective-permute-start(bf16[528,128]{1,0:T(8,128)(2,1)S(1)} %copy-done.36), channel_id=1, source_target_pairs={{0,24},{4,28},{8,0},{12,4},{16,8},{20,12},{24,16},{28,20},{1,25},{... | collective-permute-start | bytes 405512 | tf_op jit(solution)/shard_map/ppermute | solution.py:288
  151.4 20.3 %collective-permute-start.21 = (bf16[528,128]{1,0:T(8,128)(2,1)S(1)}, bf16[528,128]{1,0:T(8,128)(2,1)S(1)}, u32[]{:S(2)}, u32[]{:S(2)}) collective-permute-start(bf16[528,128]{1,0:T(8,128)(2,1)S(1)} %copy-done.35), channel_id=1, source_target_pairs={{0,16},{4,20},{8,24},{12,28},{16,0},{20,4},{24,8},{28,12},{1,17},{... | collective-permute-start | bytes 405512 | tf_op jit(solution)/shard_map/ppermute | solution.py:288
  151.4 20.3 %collective-permute-start.22 = (bf16[528,128]{1,0:T(8,128)(2,1)S(1)}, bf16[528,128]{1,0:T(8,128)(2,1)S(1)}, u32[]{:S(2)}, u32[]{:S(2)}) collective-permute-start(bf16[528,128]{1,0:T(8,128)(2,1)S(1)} %copy-done.34), channel_id=1, source_target_pairs={{0,8},{4,12},{8,16},{12,20},{16,24},{20,28},{24,0},{28,4},{1,9},{5... | collective-permute-start | bytes 405512 | tf_op jit(solution)/shard_map/ppermute | solution.py:288
  152.5 22.8 %collective-permute-start.26 = (bf16[1040,128]{1,0:T(8,128)(2,1)}, bf16[1040,128]{1,0:T(8,128)(2,1)S(1)}, u32[]{:S(2)}, u32[]{:S(2)}) collective-permute-start(bf16[1040,128]{1,0:T(8,128)(2,1)} %get-tuple-element.72), channel_id=1, source_target_pairs={{0,24},{4,28},{8,0},{12,4},{16,8},{20,12},{24,16},{28,20},{1,25},{... | collective-permute-start | bytes 798728 | tf_op jit(solution)/shard_map/ppermute | solution.py:288
  158.4 27.2 %collective-permute-start.27 = (bf16[1040,128]{1,0:T(8,128)(2,1)S(1)}, bf16[1040,128]{1,0:T(8,128)(2,1)S(1)}, u32[]{:S(2)}, u32[]{:S(2)}) collective-permute-start(bf16[1040,128]{1,0:T(8,128)(2,1)S(1)} %copy-done.33), channel_id=1, source_target_pairs={{0,16},{4,20},{8,24},{12,28},{16,0},{20,4},{24,8},{28,12},{1,17},{... | collective-permute-start | bytes 798728 | tf_op jit(solution)/shard_map/ppermute | solution.py:288
  171.7 14.0 %collective-permute-start.28 = (bf16[1040,128]{1,0:T(8,128)(2,1)S(1)}, bf16[1040,128]{1,0:T(8,128)(2,1)S(1)}, u32[]{:S(2)}, u32[]{:S(2)}) collective-permute-start(bf16[1040,128]{1,0:T(8,128)(2,1)S(1)} %copy-done.32), channel_id=1, source_target_pairs={{0,8},{4,12},{8,16},{12,20},{16,24},{20,28},{24,0},{28,4},{1,9},{5... | collective-permute-start | bytes 798728 | tf_op jit(solution)/shard_map/ppermute | solution.py:288
  (37 other events, 216.0 us)

commit v2 on v1

--- a/solution.py
+++ b/solution.py
@@ -257,12 +257,6 @@
     put(packed, 0, encode(keys[...], scaled))
 
 
-def query_kernel(queries, down, packed, down_squares):
-    put(packed, 0, encode(queries[...]))
-    squares = jnp.sum(down[...] * down[...], axis=1, keepdims=True)
-    down_squares[...] = jnp.transpose(jnp.broadcast_to(squares, (squares.shape[0], LANES)))[:1]
-
-
 def body_hidden(queries, keys, values, rates, gate_fast, up_fast, down_fast, out_proj, out_grad):
     heads = lax.axis_size("head")
     seq_count = lax.axis_size("seq")
@@ -283,27 +277,33 @@
     size_part = coded_rows(part, head_size)
     steps = range(1, depth)
 
-    def turn(array, step):
-        perm = [(s, (s + 2 * step) % seq_count) for s in range(seq_count)]
-        return lax.ppermute(array, "seq", perm)
+    def across(array, step):
+        return lax.ppermute(array, "seq", [(s, s ^ (2 * step)) for s in range(seq_count)])
 
     def swap(array):
         return lax.ppermute(array, "seq", [(s, s ^ 1) for s in range(seq_count)])
 
     def gather_z(packed):
-        return [turn(packed, step) for step in steps]
+        held, step = {0: packed}, depth // 2
+        while step:
+            for slot in sorted(held):
+                held[slot ^ step] = across(held[slot], step)
+            step //= 2
+        return [held[slot] for slot in range(1, depth)]
 
     def scatter_z(slots):
-        return [turn(packed, -step) for step, packed in zip(steps, slots)]
-
-    def sum_z(array):
-        reach = 1
-        while True:
-            other = lax.ppermute(array, "seq", [(s, s ^ (2 * reach)) for s in range(seq_count)])
-            reach *= 2
-            if reach >= depth:
-                return array, other
-            array = array + other
+        return [across(packed, step) for step, packed in zip(steps, slots)]
+
+    def sum_over(array, hops):
+        other = None
+        for hop in hops:
+            array = array if other is None else array + other
+            other = lax.ppermute(array, "seq", [(s, s ^ hop) for s in range(seq_count)])
+        return array, other
+
+    z_hops = [2 << bit for bit in range(depth.bit_length() - 1)]
+
+    spot = jnp.stack([along_z, along_y, my_head]).astype(jnp.int32)
 
     target, kv_packed = call(
         first_kernel, [((tokens, head_size), f32), ((size_two, LANES), bf16)], keys, values, rates
@@ -317,10 +317,12 @@
         perm += [(s * heads + h, (2 * h + y) * heads + lane) for h in range(heads)]
     og_mine = lax.ppermute(out_grad, ("seq", "head"), perm)
     op_other = swap(out_proj)
-    og_all = [og_mine] + [
-        lax.ppermute(og_mine, "head", [(h, (h + step) % heads) for h in range(heads)])
-        for step in range(1, heads)
-    ]
+    og_all, step = {0: og_mine}, heads // 2
+    while step:
+        for slot in sorted(og_all):
+            og_all[slot ^ step] = lax.ppermute(og_all[slot], "head", [(h, h ^ step) for h in range(heads)])
+        step //= 2
+    og_all = [og_all[slot] for slot in range(heads)]
 
     def contract_kernel(spot, mine, other, *refs):
         rows, outs, product = refs[:heads], refs[heads:-1], refs[-1]
@@ -331,15 +333,14 @@
             second = rows[k][:, pl.ds(pl.multiple_of((1 - y) * width, width), width)]
             block = lax.dot_general(first, mine[...], (NT, ((), ())), preferred_element_type=f32)
             block = block + lax.dot_general(second, other[...], (NT, ((), ())), preferred_element_type=f32)
-            lane = lax.rem(h - k + heads, heads)
+            lane = lax.bitwise_xor(h, k)
             source = lax.div(lane, 2) + lax.rem(lane, 2) * (heads // 2)
-            slot = lax.rem(z - source + depth, depth)
+            slot = lax.bitwise_xor(z, source)
             product[pl.ds(pl.multiple_of(slot * tokens, tokens), tokens), :] = block
         outs[0][...] = product[:tokens, :]
         for step in steps:
             put(outs[step], 0, encode(product[step * tokens : (step + 1) * tokens, :]))
 
-    spot = jnp.stack([along_z, along_y, my_head]).astype(jnp.int32)
     oc_own, *oc_slots = call(
         contract_kernel,
         [((tokens, head_size), f32)] + [((size_one, LANES), bf16)] * (depth - 1),
@@ -364,16 +365,27 @@
         total_kernel, [((tokens, head_size), f32), ((size_one, LANES), bf16)], oc_own, *oc_back
     )
     oc_sent = gather_z(oc_packed)
-    q_packed, down_sq = call(
-        query_kernel, [((size_one, LANES), bf16), ((1, head_size), f32)], queries, down_fast[0]
+
+    def query_kernel(spot, queries, gate, up, down, packed, weight, down_squares):
+        put(packed, 0, encode(queries[...]))
+        squares = jnp.sum(down[...] * down[...], axis=1, keepdims=True)
+        down_squares[...] = jnp.transpose(jnp.broadcast_to(squares, (squares.shape[0], LANES)))[:1]
+        start = pl.multiple_of(spot[0] * part, part)
+        weight[:part, :] = gate[pl.ds(start, part), :]
+        weight[part : 2 * part, :] = up[pl.ds(start, part), :]
+        weight[2 * part :, :] = jnp.transpose(down[:, pl.ds(start, part)])
+
+    q_packed, weights, down_sq = call(
+        query_kernel,
+        [((size_one, LANES), bf16), ((3 * part, head_size), f32), ((1, head_size), f32)],
+        spot,
+        queries,
+        gate_fast[0],
+        up_fast[0],
+        down_fast[0],
+        smem=1,
     )
     q_sent = gather_z(q_packed)
-
-    start = along_z * part
-    gate = lax.dynamic_slice_in_dim(gate_fast[0], start, part, 0)
-    up = lax.dynamic_slice_in_dim(up_fast[0], start, part, 0)
-    down = lax.dynamic_slice_in_dim(down_fast[0], start, part, 1).T
-    weights = jnp.concatenate([gate, up, down], axis=0)
 
     def update_kernel(weight, key_own, target_own, *refs):
         sent = refs[: depth - 1]
@@ -462,7 +474,7 @@
     partial, sums_own = call(
         sums_kernel, [((3 * part, head_size), f32), (sums_shape, f32)], weights, partial_own, partial_other
     )
-    sums = sum_z(sums_own)
+    sums = sum_over(sums_own, z_hops)
 
     def updated(weight, down_squares, partial, *sums):
         *totals, sq_down, cross_down = get_sums(*sums)
@@ -483,17 +495,23 @@
             found.append((matrix, grad, moved, old, new, norm))
         return found, cross_down - (scales[2] / found[2][5]) * sq_down
 
+    def moved_grad(entry, grad, along):
+        _, _, moved, old, new, _ = entry
+        return (old / new) * (grad - moved * (along / (new * new)))
+
     def apply_kernel(weight, down_squares, partial, near, far, query_own, cot_own, *refs):
         count = depth - 1
         q_refs, oc_refs, outs = refs[:count], refs[count : 2 * count], refs[2 * count :]
-        cots, packed, query_part, sent = outs[0], outs[1], outs[2], outs[3:]
+        cots, packed, inners, grads_high, grads_low, two_high, two_low = outs
         found, _ = updated(weight, down_squares, partial, near, far)
         renormed = [moved * (old / new) for _, _, moved, old, new, _ in found]
         two = split(jnp.concatenate(renormed[:2], axis=0))
         third = split(renormed[2])
+        two_high[...], two_low[...] = two
         sum_two = jnp.zeros((2 * part, head_size), f32)
         sum_one = jnp.zeros((part, head_size), f32)
-        for slot in reversed(range(depth)):
+        for slot in range(depth):
+            at = slice(slot * tokens, (slot + 1) * tokens)
             if slot == 0:
                 query_rows, cot_rows = query_own[...], cot_own[...]
             else:
@@ -505,23 +523,34 @@
             before, linear = both[:, :part], both[:, part:]
             _, act, slope = silu_parts(before)
             grads = split(jnp.concatenate([h_cot * linear * slope, h_cot * act], axis=1))
+            grads_high[at, :], grads_low[at, :] = grads
             sum_two = sum_two + dot3(grads, query_rows, TN)
             sum_one = sum_one + dot3(split(act * linear), cot_rows, TN)
-            query_rows = dot3(grads, two, NN)
-            if slot == 0:
-                query_part[...] = query_rows
-            else:
-                put(sent[slot - 1], 0, encode(query_rows))
         cots[: 2 * part, :] = sum_two
         cots[2 * part :, :] = sum_one
-        end = put(packed, 0, encode(sum_two[:part]))
-        end = put(packed, end, encode(sum_two[part:]))
-        put(packed, end, encode(sum_one))
-
-    cots_own, cots_packed, query_part, *query_slots = call(
+        found_cots = (sum_two[:part], sum_two[part:], sum_one)
+        end = 0
+        for grad in found_cots:
+            end = put(packed, end, encode(grad))
+        totals = []
+        for slot in range(2):
+            grad = found_cots[slot]
+            along = jnp.sum(found[slot][2] * grad, axis=1, keepdims=True)
+            totals.append(-whole_sum(found[slot][1] * moved_grad(found[slot], grad, along)))
+        put_sums(
+            inners,
+            totals[0],
+            totals[1],
+            jnp.zeros((1, 1), f32),
+            jnp.sum(found[2][2] * sum_one, axis=0, keepdims=True),
+            jnp.sum(found[2][1] * sum_one, axis=0, keepdims=True),
+        )
+
+    cots_own, cots_packed, inners_own, *query_parts = call(
         apply_kernel,
-        [((3 * part, head_size), f32), ((3 * size_part, LANES), bf16), ((tokens, head_size), f32)]
-        + [((size_one, LANES), bf16)] * (depth - 1),
+        [((3 * part, head_size), f32), ((3 * size_part, LANES), bf16), (sums_shape, f32)]
+        + [((depth * tokens, 2 * part), bf16)] * 2
+        + [((2 * part, head_size), bf16)] * 2,
         weights,
         down_sq,
         partial,
@@ -532,51 +561,50 @@
         *oc_sent,
     )
     cots_other = swap(cots_packed)
-
-    def moved_grad(entry, grad, along):
-        _, _, moved, old, new, _ = entry
-        return (old / new) * (grad - moved * (along / (new * new)))
-
-    def inner_kernel(weight, down_squares, partial, near, far, own, packed, cots, inners):
-        found, _ = updated(weight, down_squares, partial, near, far)
-        totals = []
-        for slot in range(3):
-            grad = add_swapped(own, packed, slot)
-            cots[slot * part : (slot + 1) * part, :] = grad
-            if slot < 2:
-                along = jnp.sum(found[slot][2] * grad, axis=1, keepdims=True)
-                totals.append(-whole_sum(found[slot][1] * moved_grad(found[slot], grad, along)))
-        put_sums(
-            inners,
-            totals[0],
-            totals[1],
-            jnp.zeros((1, 1), f32),
-            jnp.sum(found[2][2] * grad, axis=0, keepdims=True),
-            jnp.sum(found[2][1] * grad, axis=0, keepdims=True),
-        )
-
-    cots, inners_own = call(
-        inner_kernel,
-        [((3 * part, head_size), f32), (sums_shape, f32)],
-        weights,
-        down_sq,
-        partial,
-        *sums,
-        cots_own,
-        cots_other,
-    )
-    inners = sum_z(inners_own)
-
-    def second_kernel(spot, weight, down_squares, partial, near, far, cots, inner_near, inner_far, mids, *refs):
-        key_high, key_low, target_high, target_low = refs[:4]
-        key_part, target_part, mine, other, down_part = refs[4:9]
-        sent, (whole, direct_rows) = refs[9:-2], refs[-2:]
+    inners = sum_over(inners_own, z_hops + [1])
+
+    def query_back_kernel(grads_high, grads_low, two_high, two_low, query_part, *sent):
+        two = (two_high[...], two_low[...])
+        for slot in reversed(range(depth)):
+            at = slice(slot * tokens, (slot + 1) * tokens)
+            query_rows = dot3((grads_high[at, :], grads_low[at, :]), two, NN)
+            if slot == 0:
+                query_part[...] = query_rows
+            else:
+                put(sent[slot - 1], 0, encode(query_rows))
+
+    query_part, *query_slots = call(
+        query_back_kernel,
+        [((tokens, head_size), f32)] + [((size_one, LANES), bf16)] * (depth - 1),
+        *query_parts,
+    )
+    query_back = scatter_z(query_slots)
+
+    def second_slot(rows, mids, turns, matrices):
+        key_rows, target_rows = rows
+        both = dot3(key_rows, turns[0], NT)
+        c_hidden = dot3(target_rows, turns[1], NT)
+        c_bgrad, c_lgrad = both[:, :part], both[:, part:]
+        before, linear, hgrad = mids[:, :part], mids[:, part : 2 * part], mids[:, 2 * part :]
+        sigma, act, slope = silu_parts(before)
+        bend = sigma * (1.0 - sigma) * (2.0 + before * (1.0 - 2.0 * sigma))
+        c_linear = c_hidden * act + c_bgrad * hgrad * slope
+        c_hgrad = split(c_bgrad * linear * slope + c_lgrad * act)
+        c_before = c_hidden * linear * slope + c_bgrad * hgrad * linear * bend + c_lgrad * hgrad * slope
+        through = split(jnp.concatenate([c_before, c_linear], axis=1))
+        grads = split(jnp.concatenate([hgrad * linear * slope, hgrad * act], axis=1))
+        key_out = dot3(join(grads, through, axis=1), matrices[0], NN)
+        target_out = dot3(join(split(act * linear), c_hgrad, axis=1), matrices[1], NN)
+        return key_out, target_out, join(through, c_hgrad, axis=1)
+
+    def second_kernel(weight, down_squares, partial, near, far, cots, packed, inner_near, inner_far, mids, *refs):
+        kv, (turn_high, turn_low, directs, back_high, back_low, *sent) = refs[:4], refs[4:]
         found, moved_dot = updated(weight, down_squares, partial, near, far)
         inner_gate, inner_up, _, along_down, dot_down = get_sums(inner_near, inner_far)
         directions = []
         for slot in range(3):
             matrix, change, moved, old, new, norm = found[slot]
-            grad = cots[slot * part : (slot + 1) * part, :]
+            grad = add_swapped(cots, packed, slot)
             if slot < 2:
                 along = jnp.sum(moved * grad, axis=1, keepdims=True)
                 inner = (inner_gate, inner_up)[slot]
@@ -586,77 +614,106 @@
                     (old / new) * (dot_down - moved_dot * (along / (new * new))), axis=1, keepdims=True
                 )
             back = moved_grad(found[slot], grad, along)
-            direct_rows[slot * part : (slot + 1) * part, :] = back + (along / (new * old)) * matrix
+            directs[slot * part : (slot + 1) * part, :] = back + (along / (new * old)) * matrix
             directions.append((scales[slot] / norm) * (-back - change * (inner / (norm * norm))))
-        turn_two = split(jnp.concatenate(directions[:2], axis=0))
-        turn_one = split(directions[2])
-        key_matrix = join(turn_two, split(weight[: 2 * part, :]), axis=0)
-        target_matrix = join(turn_one, split(weight[2 * part :, :]), axis=0)
-        sum_two = jnp.zeros((2 * part, head_size), f32)
-        sum_one = jnp.zeros((part, head_size), f32)
-        for slot in reversed(range(depth)):
+        turns = split(jnp.concatenate(directions, axis=0))
+        turn_high[...], turn_low[...] = turns
+        steady = split(weight[...])
+        first = [tuple(side[: 2 * part] for side in pair) for pair in (turns, steady)]
+        third = [tuple(side[2 * part :] for side in pair) for pair in (turns, steady)]
+        matrices = (join(*first, axis=0), join(*third, axis=0))
+        for slot in reversed(range(1, depth)):
             at = slice(slot * tokens, (slot + 1) * tokens)
-            key_rows = (key_high[at, :], key_low[at, :])
-            target_rows = (target_high[at, :], target_low[at, :])
-            both = dot3(key_rows, turn_two, NT)
-            c_hidden = dot3(target_rows, turn_one, NT)
-            c_bgrad, c_lgrad = both[:, :part], both[:, part:]
-            before, linear = mids[at, :part], mids[at, part : 2 * part]
-            hgrad = mids[at, 2 * part :]
-            sigma, act, slope = silu_parts(before)
-            bend = sigma * (1.0 - sigma) * (2.0 + before * (1.0 - 2.0 * sigma))
-            c_linear = c_hidden * act + c_bgrad * hgrad * slope
-            c_hgrad = c_bgrad * linear * slope + c_lgrad * act
-            c_before = c_hidden * linear * slope + c_bgrad * hgrad * linear * bend + c_lgrad * hgrad * slope
-            through = split(jnp.concatenate([c_before, c_linear], axis=1))
-            grads = split(jnp.concatenate([hgrad * linear * slope, hgrad * act], axis=1))
-            c_hgrad = split(c_hgrad)
-            key_out = dot3(join(grads, through, axis=1), key_matrix, NN)
-            target_out = dot3(join(split(act * linear), c_hgrad, axis=1), target_matrix, NN)
+            rows = ((kv[0][at, :], kv[1][at, :]), (kv[2][at, :], kv[3][at, :]))
+            key_out, target_out, kept = second_slot(rows, mids[at, :], (first[0], third[0]), matrices)
+            put(sent[slot - 1], 0, encode(key_out, target_out))
+            back_high[at, :], back_low[at, :] = kept
+
+    turn_high, turn_low, directs, back_high, back_low, *grad_slots = call(
+        second_kernel,
+        [((3 * part, head_size), bf16)] * 2
+        + [((3 * part, head_size), f32)]
+        + [((depth * tokens, 3 * part), bf16)] * 2
+        + [((size_two, LANES), bf16)] * (depth - 1),
+        weights,
+        down_sq,
+        partial,
+        *sums,
+        cots_own,
+        cots_other,
+        *inners,
+        mids,
+        *kv_split,
+    )
+    grad_back = scatter_z(grad_slots)
+
+    def through_kernel(spot, weight, mids, turn_high, turn_low, directs, back_high, back_low, *refs):
+        kv, (key_part, target_part, kept_high, kept_low, down_part) = refs[:4], refs[4:]
+        turns, steady = (turn_high[...], turn_low[...]), split(weight[...])
+        first = [tuple(side[: 2 * part] for side in pair) for pair in (turns, steady)]
+        third = [tuple(side[2 * part :] for side in pair) for pair in (turns, steady)]
+        matrices = (join(*first, axis=0), join(*third, axis=0))
+        own = slice(0, tokens)
+        rows = ((kv[0][own, :], kv[1][own, :]), (kv[2][own, :], kv[3][own, :]))
+        key_part[...], target_part[...], kept = second_slot(rows, mids[own, :], (first[0], third[0]), matrices)
+        kept_high[...], kept_low[...] = kept
+        total = dot3(tuple(side[:, 2 * part :] for side in kept), rows[1], TN)
+        for slot in range(1, depth):
+            at = slice(slot * tokens, (slot + 1) * tokens)
+            kept = (back_high[at, 2 * part :], back_low[at, 2 * part :])
+            total = total + dot3(kept, (kv[2][at, :], kv[3][at, :]), TN)
+        keep = jnp.where(spot[1] == 0, 1.0, 0.0)
+        down_part[...] = jnp.transpose(total + directs[2 * part :, :] * keep)
+
+    key_part, target_part, kept_high, kept_low, down_part = call(
+        through_kernel,
+        [((tokens, head_size), f32)] * 2 + [((tokens, 3 * part), bf16)] * 2 + [((head_size, part), f32)],
+        spot,
+        weights,
+        mids,
+        turn_high,
+        turn_low,
+        directs,
+        back_high,
+        back_low,
+        *kv_split,
+        smem=1,
+    )
+    share = head_size // seq_count
+    down_all = lax.all_to_all(down_part, "seq", 0, 0, tiled=True)
+
+    def rows_kernel(spot, directs, kept_high, kept_low, back_high, back_low, key_high, key_low, mine, other, whole):
+        total = jnp.zeros((2 * part, head_size), f32)
+        for slot in range(depth):
+            at = slice(slot * tokens, (slot + 1) * tokens)
+            kept = (back_high[at, : 2 * part], back_low[at, : 2 * part])
             if slot == 0:
-                key_part[...] = key_out
-                target_part[...] = target_out
-            else:
-                put(sent[slot - 1], 0, encode(key_out, target_out))
-            sum_two = sum_two + dot3(through, key_rows, TN)
-            sum_one = sum_one + dot3(c_hgrad, target_rows, TN)
-        whole[...] = sum_two
+                kept = (kept_high[:, : 2 * part], kept_low[:, : 2 * part])
+            total = total + dot3(kept, (key_high[at, :], key_low[at, :]), TN)
+        whole[...] = total
         y = spot[1]
         near = pl.multiple_of(y * half, half)
         far = pl.multiple_of((1 - y) * half, half)
         for slot in range(2):
             rows = slice(slot * half, (slot + 1) * half)
-            mine[rows, :] = whole[pl.ds(slot * part + near, half), :] + direct_rows[pl.ds(slot * part + near, half), :]
-            other[rows, :] = whole[pl.ds(slot * part + far, half), :]
-        keep = jnp.where(y == 0, 1.0, 0.0)
-        down_part[...] = jnp.transpose(sum_one + direct_rows[2 * part :, :] * keep)
-
-    key_part, target_part, rows_mine, rows_other, down_part, *grad_slots = call(
-        second_kernel,
-        [((tokens, head_size), f32)] * 2
-        + [((2 * half, head_size), f32)] * 2
-        + [((head_size, part), f32)]
-        + [((size_two, LANES), bf16)] * (depth - 1),
+            mine[rows, :] = whole[pl.ds(slot * part + near, half), :] + directs[pl.ds(slot * part + near, half), :]
+        away = [whole[pl.ds(slot * part + far, half), :] for slot in range(2)]
+        put(other, 0, encode(jnp.concatenate(away, axis=0)))
+
+    rows_mine, rows_other = call(
+        rows_kernel,
+        [((2 * half, head_size), f32), ((size_part, LANES), bf16)],
         spot,
-        weights,
-        down_sq,
-        partial,
-        *sums,
-        cots,
-        *inners,
-        mids,
-        *kv_split,
-        scratch=[pltpu.VMEM((2 * part, head_size), f32), pltpu.VMEM((3 * part, head_size), f32)],
+        directs,
+        kept_high,
+        kept_low,
+        back_high,
+        back_low,
+        *kv_split[:2],
+        scratch=[pltpu.VMEM((2 * part, head_size), f32)],
         smem=1,
     )
-    grad_back = scatter_z(grad_slots)
-    rows_out = (rows_mine + swap(rows_other)).reshape(2, half, head_size)
-    share = head_size // seq_count
-    down_all = lax.all_to_all(down_part, "seq", 0, 0, tiled=True)
-    down_all = down_all.reshape(depth, 2, share, part).sum(axis=1)
-    down_out = down_all.transpose(1, 0, 2).reshape(share, hidden_size)
-
-    query_back = scatter_z(query_slots)
+    rows_back = swap(rows_other)
 
     def query_end_kernel(own, *refs):
         value = own[...]
@@ -665,6 +722,24 @@
         refs[-1][...] = value
 
     (query_grad,) = call(query_end_kernel, [((tokens, head_size), f32)], query_part, *query_back)
+
+    def finish_kernel(rows_mine, rows_back, down_all, gate_out, up_out, down_out):
+        rows = rows_mine[...] + decode(rows_back, 0, 2 * half, head_size)[0]
+        gate_out[0] = rows[:half]
+        up_out[0] = rows[half:]
+        for z in range(depth):
+            at = 2 * z * share
+            down_out[0, :, z * part : (z + 1) * part] = (
+                down_all[at : at + share, :] + down_all[at + share : at + 2 * share, :]
+            )
+
+    gate_grad, up_grad, down_grad = call(
+        finish_kernel,
+        [((1, half, head_size), f32)] * 2 + [((1, share, hidden_size), f32)],
+        rows_mine,
+        rows_back,
+        down_all,
+    )
 
     def end_kernel(rates, key_own, target_own, *refs):
         sent, (key_out, value_out) = refs[: depth - 1], refs[depth - 1 :]
@@ -678,7 +753,7 @@
     key_grad, value_grad = call(
         end_kernel, [((tokens, head_size), f32)] * 2, rates, key_part, target_part, *grad_back
     )
-    return (query_grad, key_grad, value_grad, rows_out[0][None], rows_out[1][None], down_out[None])
+    return query_grad, key_grad, value_grad, gate_grad, up_grad, down_grad
 
 
 def fits_hidden(mesh, tokens, hidden, head_size, heads):

time: 193 us -> 183 us (0.948)
  the two profiles are of different devices: /device:TPU:0 before, /device:TPU:10 now
where the time goes in v2:
time: 183 us; the launch traced here: 182 us
  waiting for transfers between devices  71.3 us (39%)
  Pallas kernels  53.3 us (29%)
  starting transfers between devices  47.4 us (26%)
  local copies, waits for them, and re-layouts  7.46 us (4%)
  other arithmetic  2 us (1%)
    pallas_call x14, Pallas kernels, call(): pl.pallas_call(kernel, out_shape=[jax.ShapeDtypeStruct(shape, dtype) for...  53.3 us
    ppermute x18, waiting for transfers between devices, across(): lax.ppermute(array, 'seq', [(s, s ^ 2 * step) for s in range(seq_count)])  42.4 us
    ppermute x18, starting transfers between devices, across(): lax.ppermute(array, 'seq', [(s, s ^ 2 * step) for s in range(seq_count)])  24.1 us
    ppermute x1, waiting for transfers between devices, body_hidden(): og_mine = lax.ppermute(out_grad, ('seq', 'head'), perm)  13.2 us
    ppermute x5, waiting for transfers between devices, sum_over(): other = lax.ppermute(array, 'seq', [(s, s ^ hop) for s in range(seq_count)])  12.9 us
    ppermute x5, starting transfers between devices, sum_over(): other = lax.ppermute(array, 'seq', [(s, s ^ hop) for s in range(seq_count)])  8.48 us
    unnamed x72, local copies, waits for them, and re-layouts  7.46 us
    all_to_all x1, starting transfers between devices, body_hidden(): down_all = lax.all_to_all(down_part, 'seq', 0, 0, tiled=True)  5.57 us
  transfers between devices with their start and end apart: 32, of which 14 were waited for; matrix products, arithmetic and copies ran while one was open for 1% of the time, Pallas kernels for 18%

profile of v2, /device:TPU:10, one launch (start us, length us, event | category | flops | bytes accessed | tf_op | source)
XLA Modules:
  0.0 182.4 jit_solution(3933878118720282042)
XLA Ops:
  0.6 3.6 %collective-permute-start.7 = (bf16[128,1024]{1,0:T(8,128)(2,1)}, bf16[128,1024]{1,0:T(8,128)(2,1)S(1)}, u32[]{:S(2)}, u32[]{:S(2)}) collective-permute-start(bf16[128,1024]{1,0:T(8,128)(2,1)} %param.17), channel_id=1, source_target_pairs={{0,0},{1,8},{2,16},{3,24},{4,4},{5,12},{6,20},{7,28},{8,2},{9,10},... | collective-permute-start | bytes 786440 | tf_op jit(solution)/shard_map/ppermute | solution.py:318
  4.3 2.2 %shard_map.137 = (f32[128,512]{1,0:T(8,128)}, bf16[1040,128]{1,0:T(8,128)(2,1)}) custom-call(f32[128,512]{1,0:T(8,128)} %key_own.1, f32[128,512]{1,0:T(8,128)} %values.1, f32[1,128]{1,0:T(1,128)} %rates.3), custom_call_target="tpu_custom_call" | custom-call | tf_op jit(solution)/shard_map/pallas_call | solution.py:245
  9.0 13.2 %collective-permute-done.7.refs_0_ = bf16[128,1024]{1,0:T(8,128)(2,1)S(1)} collective-permute-done((bf16[128,1024]{1,0:T(8,128)(2,1)}, bf16[128,1024]{1,0:T(8,128)(2,1)S(1)}, u32[]{:S(2)}, u32[]{:S(2)}) %collective-permute-start.7) | collective-permute-done | bytes 262176 | tf_op jit(solution)/shard_map/ppermute | solution.py:318
  22.2 5.7 %collective-permute-done.1.refs_1_ = bf16[1040,128]{1,0:T(8,128)(2,1)S(1)} collective-permute-done((bf16[1040,128]{1,0:T(8,128)(2,1)}, bf16[1040,128]{1,0:T(8,128)(2,1)S(1)}, u32[]{:S(2)}, u32[]{:S(2)}) %collective-permute-start.1) | collective-permute-done | bytes 266272 | tf_op jit(solution)/shard_map/ppermute | solution.py:281
  28.5 2.9 %collective-permute-done.9.refs_2_ = bf16[128,1024]{1,0:T(8,128)(2,1)S(1)} collective-permute-done((bf16[128,1024]{1,0:T(8,128)(2,1)S(1)}, bf16[128,1024]{1,0:T(8,128)(2,1)S(1)}, u32[]{:S(2)}, u32[]{:S(2)}) %collective-permute-start.9) | collective-permute-done | bytes 262176 | tf_op jit(solution)/shard_map/ppermute | solution.py:323
  32.0 3.3 %shard_map.136 = (bf16[528,128]{1,0:T(8,128)(2,1)}, f32[384,512]{1,0:T(8,128)}, f32[1,512]{1,0:T(1,128)}) custom-call(s32[3]{0:T(128)} %pad_add_fusion.spot, f32[128,512]{1,0:T(8,128)} %query_own.1, f32[512,512]{1,0:T(8,128)} %bitcast.8, f32[512,512]{1,0:T(8,128)} %bitcast.9, f32[512,512]{1,0:T(8,128)} %bitcast.10), custom_call_target="tpu_custom_call" | custom-call | tf_op jit(solution)/shard_map/pallas_call | solution.py:245
  38.0 6.7 %shard_map.138 = (bf16[512,512]{1,0:T(8,128)(2,1)}, bf16[512,512]{1,0:T(8,128)(2,1)}, bf16[512,512]{1,0:T(8,128)(2,1)}, bf16[512,512]{1,0:T(8,128)(2,1)}, f32[51...) custom-call(f32[384,512]{1,0:T(8,128)} %get-tuple-element.57.weight, f32[128,512]{1,0:T(8,128)} %key_own.1, ...), custom_call_target="tpu_custom_call" | custom-call | tf_op jit(solution)/shard_map/pallas_call | solution.py:245
  47.8 4.0 %shard_map.140 = (f32[128,512]{1,0:T(8,128)}, bf16[528,128]{1,0:T(8,128)(2,1)}, bf16[528,128]{1,0:T(8,128)(2,1)}, bf16[528,128]{1,0:T(8,128)(2,1)}) custom-call(s32[3]{0:T(128)} %pad_add_fusion.spot, bf16[512,512]{1,0:T(8,128)(2,1)} %mine.1, bf16[512,512]{1,0:T(8,128)(2,1)} %copy-done.2, bf16[128,1024]{1,0:T(8,128)(2,1)} %copy-done.11, ...), custom_call_target="tpu_custom_call" | custom-call | tf_op jit(solution)/shard_map/pallas_call | solution.py:245
  51.9 5.0 %collective-permute-start.12 = (bf16[528,128]{1,0:T(8,128)(2,1)}, bf16[528,128]{1,0:T(8,128)(2,1)S(1)}, u32[]{:S(2)}, u32[]{:S(2)}) collective-permute-start(bf16[528,128]{1,0:T(8,128)(2,1)} %get-tuple-element.67), channel_id=1, source_target_pairs={{0,16},{4,20},{8,24},{12,28},{16,0},{20,4},{24,8},{28,12},{1,17},{... | collective-permute-start | bytes 405512 | tf_op jit(solution)/shard_map/ppermute | solution.py:281
  57.5 3.8 %collective-permute-start.15 = (bf16[528,128]{1,0:T(8,128)(2,1)S(1)}, bf16[528,128]{1,0:T(8,128)(2,1)S(1)}, u32[]{:S(2)}, u32[]{:S(2)}) collective-permute-start(bf16[528,128]{1,0:T(8,128)(2,1)S(1)} %copy-done.35), channel_id=1, source_target_pairs={{0,16},{4,20},{8,24},{12,28},{16,0},{20,4},{24,8},{28,12},{1,17},{... | collective-permute-start | bytes 405512 | tf_op jit(solution)/shard_map/ppermute | solution.py:281
  61.3 8.0 %collective-permute-done.12.refs_1_ = bf16[528,128]{1,0:T(8,128)(2,1)S(1)} collective-permute-done((bf16[528,128]{1,0:T(8,128)(2,1)}, bf16[528,128]{1,0:T(8,128)(2,1)S(1)}, u32[]{:S(2)}, u32[]{:S(2)}) %collective-permute-start.12) | collective-permute-done | bytes 135200 | tf_op jit(solution)/shard_map/ppermute | solution.py:281
  69.3 4.0 %collective-permute-done.13.refs_2_ = bf16[528,128]{1,0:T(8,128)(2,1)S(1)} collective-permute-done((bf16[528,128]{1,0:T(8,128)(2,1)}, bf16[528,128]{1,0:T(8,128)(2,1)S(1)}, u32[]{:S(2)}, u32[]{:S(2)}) %collective-permute-start.13) | collective-permute-done | bytes 135200 | tf_op jit(solution)/shard_map/ppermute | solution.py:281
  73.9 2.2 %shard_map.141 = (f32[128,512]{1,0:T(8,128)}, bf16[528,128]{1,0:T(8,128)(2,1)}) custom-call(f32[128,512]{1,0:T(8,128)} %get-tuple-element.65.own, bf16[528,128]{1,0:T(8,128)(2,1)} %copy-done.25, bf16[528,128]{1,0:T(8,128)(2,1)} %copy-done.26, bf16[528,128]{1,0:T(8,128)(2,1)} %copy-done.27), custom_call_target="tpu_custom_call" | custom-call | tf_op jit(solution)/shard_map/pallas_call | solution.py:245
  76.1 2.8 %collective-permute-start.14 = (bf16[528,128]{1,0:T(8,128)(2,1)S(1)}, bf16[528,128]{1,0:T(8,128)(2,1)S(1)}, u32[]{:S(2)}, u32[]{:S(2)}) collective-permute-start(bf16[528,128]{1,0:T(8,128)(2,1)S(1)} %copy-done.35), channel_id=1, source_target_pairs={{0,8},{4,12},{8,0},{12,4},{16,24},{20,28},{24,16},{28,20},{1,9},{5... | collective-permute-start | bytes 405512 | tf_op jit(solution)/shard_map/ppermute | solution.py:281
  80.9 2.8 %collective-permute-done.18.refs_4_ = bf16[528,128]{1,0:T(8,128)(2,1)S(1)} collective-permute-done((bf16[528,128]{1,0:T(8,128)(2,1)}, bf16[528,128]{1,0:T(8,128)(2,1)S(1)}, u32[]{:S(2)}, u32[]{:S(2)}) %collective-permute-start.18) | collective-permute-done | bytes 135200 | tf_op jit(solution)/shard_map/ppermute | solution.py:281
  84.5 2.8 %shard_map.139 = (f32[384,512]{1,0:T(8,128)}, f32[16,128]{1,0:T(8,128)}) custom-call(f32[384,512]{1,0:T(8,128)} %get-tuple-element.57.weight, f32[384,512]{1,0:T(8,128)} %get-tuple-element.61.own, bf16[1584,128]{1,0:T(8,128)(2,1)} %copy-done.4), custom_call_target="tpu_custom_call" | custom-call | tf_op jit(solution)/shard_map/pallas_call | solution.py:245
  89.3 2.7 %collective-permute-done.4 = f32[16,128]{1,0:T(8,128)S(1)} collective-permute-done((f32[16,128]{1,0:T(8,128)}, f32[16,128]{1,0:T(8,128)S(1)}, u32[]{:S(2)}, u32[]{:S(2)}) %collective-permute-start.4) | collective-permute-done | bytes 8224 | tf_op jit(solution)/shard_map/ppermute | solution.py:301
  94.6 2.7 %collective-permute-done.5.far = f32[16,128]{1,0:T(8,128)S(1)} collective-permute-done((f32[16,128]{1,0:T(8,128)S(1)}, f32[16,128]{1,0:T(8,128)S(1)}, u32[]{:S(2)}, u32[]{:S(2)}) %collective-permute-start.5) | collective-permute-done | bytes 8224 | tf_op jit(solution)/shard_map/ppermute | solution.py:301
  98.0 7.0 %shard_map.142 = (f32[384,512]{1,0:T(8,128)}, bf16[1584,128]{1,0:T(8,128)(2,1)}, f32[16,128]{1,0:T(8,128)}, bf16[512,256]{1,0:T(8,128)(2,1)}, bf16[512,256]{1,0:...) custom-call(f32[384,512]{1,0:T(8,128)} %get-tuple-element.57.weight, ...), custom_call_target="tpu_custom_call" | custom-call | tf_op jit(solution)/shard_map/pallas_call | solution.py:245
  106.6 2.7 %collective-permute-done.24 = f32[16,128]{1,0:T(8,128)S(1)} collective-permute-done((f32[16,128]{1,0:T(8,128)}, f32[16,128]{1,0:T(8,128)S(1)}, u32[]{:S(2)}, u32[]{:S(2)}) %collective-permute-start.24) | collective-permute-done | bytes 8224 | tf_op jit(solution)/shard_map/ppermute | solution.py:301
  111.9 2.7 %collective-permute-done.25 = f32[16,128]{1,0:T(8,128)S(1)} collective-permute-done((f32[16,128]{1,0:T(8,128)S(1)}, f32[16,128]{1,0:T(8,128)S(1)}, u32[]{:S(2)}, u32[]{:S(2)}) %collective-permute-start.25) | collective-permute-done | bytes 8224 | tf_op jit(solution)/shard_map/ppermute | solution.py:301
  116.1 2.1 %collective-permute-done.26.inner_far = f32[16,128]{1,0:T(8,128)S(1)} collective-permute-done((f32[16,128]{1,0:T(8,128)S(1)}, f32[16,128]{1,0:T(8,128)S(1)}, u32[]{:S(2)}, u32[]{:S(2)}) %collective-permute-start.26) | collective-permute-done | bytes 8224 | tf_op jit(solution)/shard_map/ppermute | solution.py:301
  119.0 7.2 %shard_map.145 = (bf16[384,512]{1,0:T(8,128)(2,1)}, bf16[384,512]{1,0:T(8,128)(2,1)}, f32[384,512]{1,0:T(8,128)}, bf16[512,384]{1,0:T(8,128)(2,1)}, bf16[512,384...) custom-call(f32[384,512]{1,0:T(8,128)} %get-tuple-element.57.weight, ...), custom_call_target="tpu_custom_call" | custom-call | tf_op jit(solution)/shard_map/pallas_call | solution.py:245
  126.2 4.9 %shard_map.146 = (f32[128,512]{1,0:T(8,128)}, f32[128,512]{1,0:T(8,128)}, bf16[128,384]{1,0:T(8,128)(2,1)}, bf16[128,384]{1,0:T(8,128)(2,1)}, f32[512,128]{1,0:T(8,128)}) custom-call(s32[3]{0:T(128)} %pad_add_fusion.spot, f32[384,512]{1,0:T(8,128)} %get-tuple-element.57.weight, f32[512,384]{1,0:T(8,128)} %get-tuple-element.80.mids, ...), custom_call_target="tpu_custom_call" | custom-call | tf_op jit(solution)/shard_map/pallas_call | solution.py:245
  131.1 5.6 %all-to-all-start = ((f32[8,64,128]{2,1,0:T(8,128)}), f32[8,64,128]{2,1,0:T(8,128)S(1)}, u32[]{:S(2)}, u32[]{:S(2)}) async-start(f32[8,64,128]{2,1,0:T(8,128)} %bitcast.12), calls=%async_computation | async-start | bytes 524288 | tf_op jit(solution)/shard_map/all_to_all | solution.py:683
  136.7 2.7 %shard_map.143 = (f32[128,512]{1,0:T(8,128)}, bf16[528,128]{1,0:T(8,128)(2,1)}, bf16[528,128]{1,0:T(8,128)(2,1)}, bf16[528,128]{1,0:T(8,128)(2,1)}) custom-call(bf16[512,256]{1,0:T(8,128)(2,1)} %get-tuple-element.72.grads_high, bf16[512,256]{1,0:T(8,128)(2,1)} %get-tuple-element.73.grads_low, bf16[256,512]{1,0:T(8,128)(2,1)} %get-tuple-element.74.two_high, ...), custom_call_target="tpu_custom_call" | custom-call | tf_op jit(solution)/shard_map/pallas_call | solution.py:245
  139.4 2.9 %collective-permute-start.21 = (bf16[528,128]{1,0:T(8,128)(2,1)}, bf16[528,128]{1,0:T(8,128)(2,1)S(1)}, u32[]{:S(2)}, u32[]{:S(2)}) collective-permute-start(bf16[528,128]{1,0:T(8,128)(2,1)} %get-tuple-element.78), channel_id=1, source_target_pairs={{0,16},{4,20},{8,24},{12,28},{16,0},{20,4},{24,8},{28,12},{1,17},{... | collective-permute-start | bytes 405512 | tf_op jit(solution)/shard_map/ppermute | solution.py:281
  146.0 2.5 %collective-permute-start.22 = (bf16[528,128]{1,0:T(8,128)(2,1)}, bf16[528,128]{1,0:T(8,128)(2,1)S(1)}, u32[]{:S(2)}, u32[]{:S(2)}) collective-permute-start(bf16[528,128]{1,0:T(8,128)(2,1)} %get-tuple-element.79), channel_id=1, source_target_pairs={{0,24},{4,28},{8,16},{12,20},{16,8},{20,12},{24,0},{28,4},{1,25},{... | collective-permute-start | bytes 405512 | tf_op jit(solution)/shard_map/ppermute | solution.py:281
  148.5 3.6 %shard_map.148 = (f32[128,512]{1,0:T(8,128)}, bf16[528,128]{1,0:T(8,128)(2,1)}) custom-call(s32[3]{0:T(128)} %pad_add_fusion.spot, f32[384,512]{1,0:T(8,128)} %get-tuple-element.90.directs, bf16[128,384]{1,0:T(8,128)(2,1)} %get-tuple-element.100.kept_high, bf16[128,384]{1,0:T(8,128)(2,1)} %get-tuple-element.101.kept_low, ...), custom_call_target="tpu_custom_call" | custom-call | tf_op jit(solution)/shard_map/pallas_call | solution.py:245
  153.6 19.7 %collective-permute-done.22.refs_2_ = bf16[528,128]{1,0:T(8,128)(2,1)S(1)} collective-permute-done((bf16[528,128]{1,0:T(8,128)(2,1)}, bf16[528,128]{1,0:T(8,128)(2,1)S(1)}, u32[]{:S(2)}, u32[]{:S(2)}) %collective-permute-start.22) | collective-permute-done | bytes 135200 | tf_op jit(solution)/shard_map/ppermute | solution.py:281
  173.9 2.1 %shard_map.144 = f32[128,512]{1,0:T(8,128)} custom-call(f32[128,512]{1,0:T(8,128)} %get-tuple-element.76.own, bf16[528,128]{1,0:T(8,128)(2,1)} %copy-done.21, bf16[528,128]{1,0:T(8,128)(2,1)} %copy-done.22, bf16[528,128]{1,0:T(8,128)(2,1)} %copy-done.24), custom_call_target="tpu_custom_call" | custom-call | tf_op jit(solution)/shard_map/pallas_call | solution.py:245
  177.0 2.6 %shard_map.147 = (f32[128,512]{1,0:T(8,128)}, f32[128,512]{1,0:T(8,128)}) custom-call(f32[1,128]{1,0:T(1,128)} %rates.3, f32[128,512]{1,0:T(8,128)} %get-tuple-element.93.key_own, f32[128,512]{1,0:T(8,128)} %get-tuple-element.94.target_own, bf16[1040,128]{1,0:T(8,128)(2,1)} %copy-done.5, bf16[1040,128]{1,0:T(8,128)(2,1)} %copy-done.6, ...), custom_call_target="tpu_custom_call" | custom-call | tf_op jit(solution)/shard_map/pallas_call | solution.py:245
  (122 shorter events, 35.0 us)
Async XLA Ops:
  0.6 21.5 %collective-permute-start.7 = (bf16[128,1024]{1,0:T(8,128)(2,1)}, bf16[128,1024]{1,0:T(8,128)(2,1)S(1)}, u32[]{:S(2)}, u32[]{:S(2)}) collective-permute-start(bf16[128,1024]{1,0:T(8,128)(2,1)} %param.17), channel_id=1, source_target_pairs={{0,0},{1,8},{2,16},{3,24},{4,4},{5,12},{6,20},{7,28},{8,2},{9,10},... | collective-permute-start | bytes 786440 | tf_op jit(solution)/shard_map/ppermute | solution.py:318
  6.4 21.5 %collective-permute-start.1 = (bf16[1040,128]{1,0:T(8,128)(2,1)}, bf16[1040,128]{1,0:T(8,128)(2,1)S(1)}, u32[]{:S(2)}, u32[]{:S(2)}) collective-permute-start(bf16[1040,128]{1,0:T(8,128)(2,1)} %get-tuple-element.60), channel_id=1, source_target_pairs={{0,16},{4,20},{8,24},{12,28},{16,0},{20,4},{24,8},{28,12},{1,17},{... | collective-permute-start | bytes 798728 | tf_op jit(solution)/shard_map/ppermute | solution.py:281
  7.5 38.8 %collective-permute-start.6 = (bf16[512,512]{1,0:T(8,128)(2,1)S(1)}, bf16[512,512]{1,0:T(8,128)(2,1)S(1)}, u32[]{:S(2)}, u32[]{:S(2)}) collective-permute-start(bf16[512,512]{1,0:T(8,128)(2,1)S(1)} %copy-done.1), channel_id=1, source_target_pairs={{0,4},{4,0},{8,12},{12,8},{16,20},{20,16},{24,28},{28,24},{1,5},{5... | collective-permute-start | bytes 1572872 | tf_op jit(solution)/shard_map/ppermute | solution.py:284
  22.1 9.2 %collective-permute-start.9 = (bf16[128,1024]{1,0:T(8,128)(2,1)S(1)}, bf16[128,1024]{1,0:T(8,128)(2,1)S(1)}, u32[]{:S(2)}, u32[]{:S(2)}) collective-permute-start(bf16[128,1024]{1,0:T(8,128)(2,1)S(1)} %collective-permute-done.7.refs_0_), channel_id=1, source_target_pairs={{0,2},{1,3},{2,0},{3,1},{4,6},{5,7},{6,4},{7,5},{8,10},{9,11},{10,... | collective-permute-start | bytes 786440 | tf_op jit(solution)/shard_map/ppermute | solution.py:323
  22.2 13.2 %collective-permute-start = (bf16[1040,128]{1,0:T(8,128)(2,1)}, bf16[1040,128]{1,0:T(8,128)(2,1)S(1)}, u32[]{:S(2)}, u32[]{:S(2)}) collective-permute-start(bf16[1040,128]{1,0:T(8,128)(2,1)} %get-tuple-element.60), channel_id=1, source_target_pairs={{0,8},{4,12},{8,0},{12,4},{16,24},{20,28},{24,16},{28,20},{1,9},{5... | collective-permute-start | bytes 798728 | tf_op jit(solution)/shard_map/ppermute | solution.py:281
  27.9 9.4 %collective-permute-start.2 = (bf16[1040,128]{1,0:T(8,128)(2,1)S(1)}, bf16[1040,128]{1,0:T(8,128)(2,1)S(1)}, u32[]{:S(2)}, u32[]{:S(2)}) collective-permute-start(bf16[1040,128]{1,0:T(8,128)(2,1)S(1)} %collective-permute-done.1.refs_1_), channel_id=1, source_target_pairs={{0,8},{4,12},{8,0},{12,4},{16,24},{20,28},{24,16},{28,20},{1,9},{5... | collective-permute-start | bytes 798728 | tf_op jit(solution)/shard_map/ppermute | solution.py:281
  27.9 18.3 %collective-permute-start.8 = (bf16[128,1024]{1,0:T(8,128)(2,1)S(1)}, bf16[128,1024]{1,0:T(8,128)(2,1)S(1)}, u32[]{:S(2)}, u32[]{:S(2)}) collective-permute-start(bf16[128,1024]{1,0:T(8,128)(2,1)S(1)} %collective-permute-done.7.refs_0_), channel_id=1, source_target_pairs={{0,1},{1,0},{2,3},{3,2},{4,5},{5,4},{6,7},{7,6},{8,9},{9,8},{10,11... | collective-permute-start | bytes 786440 | tf_op jit(solution)/shard_map/ppermute | solution.py:323
  31.3 15.0 %collective-permute-start.10 = (bf16[128,1024]{1,0:T(8,128)(2,1)S(1)}, bf16[128,1024]{1,0:T(8,128)(2,1)S(1)}, u32[]{:S(2)}, u32[]{:S(2)}) collective-permute-start(bf16[128,1024]{1,0:T(8,128)(2,1)S(1)} %collective-permute-done.9.refs_2_), channel_id=1, source_target_pairs={{0,1},{1,0},{2,3},{3,2},{4,5},{5,4},{6,7},{7,6},{8,9},{9,8},{10,11... | collective-permute-start | bytes 786440 | tf_op jit(solution)/shard_map/ppermute | solution.py:323
  44.7 39.0 %collective-permute-start.3 = (bf16[1584,128]{1,0:T(8,128)(2,1)}, bf16[1584,128]{1,0:T(8,128)(2,1)S(1)}, u32[]{:S(2)}, u32[]{:S(2)}) collective-permute-start(bf16[1584,128]{1,0:T(8,128)(2,1)} %get-tuple-element.62), channel_id=1, source_target_pairs={{0,4},{4,0},{8,12},{12,8},{16,20},{20,16},{24,28},{28,24},{1,5},{5... | collective-permute-start | bytes 1216520 | tf_op jit(solution)/shard_map/ppermute | solution.py:284
  51.9 9.4 %collective-permute-start.11 = (bf16[528,128]{1,0:T(8,128)(2,1)}, bf16[528,128]{1,0:T(8,128)(2,1)S(1)}, u32[]{:S(2)}, u32[]{:S(2)}) collective-permute-start(bf16[528,128]{1,0:T(8,128)(2,1)} %get-tuple-element.66), channel_id=1, source_target_pairs={{0,8},{4,12},{8,0},{12,4},{16,24},{20,28},{24,16},{28,20},{1,9},{5... | collective-permute-start | bytes 405512 | tf_op jit(solution)/shard_map/ppermute | solution.py:281
  51.9 17.4 %collective-permute-start.12 = (bf16[528,128]{1,0:T(8,128)(2,1)}, bf16[528,128]{1,0:T(8,128)(2,1)S(1)}, u32[]{:S(2)}, u32[]{:S(2)}) collective-permute-start(bf16[528,128]{1,0:T(8,128)(2,1)} %get-tuple-element.67), channel_id=1, source_target_pairs={{0,16},{4,20},{8,24},{12,28},{16,0},{20,4},{24,8},{28,12},{1,17},{... | collective-permute-start | bytes 405512 | tf_op jit(solution)/shard_map/ppermute | solution.py:281
  56.9 16.3 %collective-permute-start.13 = (bf16[528,128]{1,0:T(8,128)(2,1)}, bf16[528,128]{1,0:T(8,128)(2,1)S(1)}, u32[]{:S(2)}, u32[]{:S(2)}) collective-permute-start(bf16[528,128]{1,0:T(8,128)(2,1)} %get-tuple-element.68), channel_id=1, source_target_pairs={{0,24},{4,28},{8,16},{12,20},{16,8},{20,12},{24,0},{28,4},{1,25},{... | collective-permute-start | bytes 405512 | tf_op jit(solution)/shard_map/ppermute | solution.py:281
  57.5 21.4 %collective-permute-start.15 = (bf16[528,128]{1,0:T(8,128)(2,1)S(1)}, bf16[528,128]{1,0:T(8,128)(2,1)S(1)}, u32[]{:S(2)}, u32[]{:S(2)}) collective-permute-start(bf16[528,128]{1,0:T(8,128)(2,1)S(1)} %copy-done.35), channel_id=1, source_target_pairs={{0,16},{4,20},{8,24},{12,28},{16,0},{20,4},{24,8},{28,12},{1,17},{... | collective-permute-start | bytes 405512 | tf_op jit(solution)/shard_map/ppermute | solution.py:281
  76.1 7.6 %collective-permute-start.18 = (bf16[528,128]{1,0:T(8,128)(2,1)}, bf16[528,128]{1,0:T(8,128)(2,1)S(1)}, u32[]{:S(2)}, u32[]{:S(2)}) collective-permute-start(bf16[528,128]{1,0:T(8,128)(2,1)} %get-tuple-element.71), channel_id=1, source_target_pairs={{0,16},{4,20},{8,24},{12,28},{16,0},{20,4},{24,8},{28,12},{1,17},{... | collective-permute-start | bytes 405512 | tf_op jit(solution)/shard_map/ppermute | solution.py:281
  76.1 18.5 %collective-permute-start.14 = (bf16[528,128]{1,0:T(8,128)(2,1)S(1)}, bf16[528,128]{1,0:T(8,128)(2,1)S(1)}, u32[]{:S(2)}, u32[]{:S(2)}) collective-permute-start(bf16[528,128]{1,0:T(8,128)(2,1)S(1)} %copy-done.35), channel_id=1, source_target_pairs={{0,8},{4,12},{8,0},{12,4},{16,24},{20,28},{24,16},{28,20},{1,9},{5... | collective-permute-start | bytes 405512 | tf_op jit(solution)/shard_map/ppermute | solution.py:281
  78.9 15.7 %collective-permute-start.16 = (bf16[528,128]{1,0:T(8,128)(2,1)S(1)}, bf16[528,128]{1,0:T(8,128)(2,1)S(1)}, u32[]{:S(2)}, u32[]{:S(2)}) collective-permute-start(bf16[528,128]{1,0:T(8,128)(2,1)S(1)} %collective-permute-done.15.refs_1_), channel_id=1, source_target_pairs={{0,8},{4,12},{8,0},{12,4},{16,24},{20,28},{24,16},{28,20},{1,9},{5... | collective-permute-start | bytes 405512 | tf_op jit(solution)/shard_map/ppermute | solution.py:281
  79.0 18.3 %collective-permute-start.17 = (bf16[528,128]{1,0:T(8,128)(2,1)}, bf16[528,128]{1,0:T(8,128)(2,1)S(1)}, u32[]{:S(2)}, u32[]{:S(2)}) collective-permute-start(bf16[528,128]{1,0:T(8,128)(2,1)} %get-tuple-element.71), channel_id=1, source_target_pairs={{0,8},{4,12},{8,0},{12,4},{16,24},{20,28},{24,16},{28,20},{1,9},{5... | collective-permute-start | bytes 405512 | tf_op jit(solution)/shard_map/ppermute | solution.py:281
  83.7 13.6 %collective-permute-start.19 = (bf16[528,128]{1,0:T(8,128)(2,1)S(1)}, bf16[528,128]{1,0:T(8,128)(2,1)S(1)}, u32[]{:S(2)}, u32[]{:S(2)}) collective-permute-start(bf16[528,128]{1,0:T(8,128)(2,1)S(1)} %collective-permute-done.18.refs_4_), channel_id=1, source_target_pairs={{0,8},{4,12},{8,0},{12,4},{16,24},{20,28},{24,16},{28,20},{1,9},{5... | collective-permute-start | bytes 405512 | tf_op jit(solution)/shard_map/ppermute | solution.py:281
  87.3 4.8 %collective-permute-start.4 = (f32[16,128]{1,0:T(8,128)}, f32[16,128]{1,0:T(8,128)S(1)}, u32[]{:S(2)}, u32[]{:S(2)}) collective-permute-start(f32[16,128]{1,0:T(8,128)} %get-tuple-element.64), channel_id=1, source_target_pairs={{0,8},{4,12},{8,0},{12,4},{16,24},{20,28},{24,16},{28,20},{1,9},{5... | collective-permute-start | bytes 24584 | tf_op jit(solution)/shard_map/ppermute | solution.py:301
  92.7 4.5 %collective-permute-start.5 = (f32[16,128]{1,0:T(8,128)S(1)}, f32[16,128]{1,0:T(8,128)S(1)}, u32[]{:S(2)}, u32[]{:S(2)}) collective-permute-start(f32[16,128]{1,0:T(8,128)S(1)} %add.15.near), channel_id=1, source_target_pairs={{0,16},{4,20},{8,24},{12,28},{16,0},{20,4},{24,8},{28,12},{1,17},{... | collective-permute-start | bytes 24584 | tf_op jit(solution)/shard_map/ppermute | solution.py:301
  105.0 13.3 %collective-permute-start.23 = (bf16[1584,128]{1,0:T(8,128)(2,1)}, bf16[1584,128]{1,0:T(8,128)(2,1)S(1)}, u32[]{:S(2)}, u32[]{:S(2)}) collective-permute-start(bf16[1584,128]{1,0:T(8,128)(2,1)} %get-tuple-element.82), channel_id=1, source_target_pairs={{0,4},{4,0},{8,12},{12,8},{16,20},{20,16},{24,28},{28,24},{1,5},{5... | collective-permute-start | bytes 1216520 | tf_op jit(solution)/shard_map/ppermute | solution.py:284
  105.5 3.9 %collective-permute-start.24 = (f32[16,128]{1,0:T(8,128)}, f32[16,128]{1,0:T(8,128)S(1)}, u32[]{:S(2)}, u32[]{:S(2)}) collective-permute-start(f32[16,128]{1,0:T(8,128)} %get-tuple-element.83), channel_id=1, source_target_pairs={{0,8},{4,12},{8,0},{12,4},{16,24},{20,28},{24,16},{28,20},{1,9},{5... | collective-permute-start | bytes 24584 | tf_op jit(solution)/shard_map/ppermute | solution.py:301
  110.0 4.5 %collective-permute-start.25 = (f32[16,128]{1,0:T(8,128)S(1)}, f32[16,128]{1,0:T(8,128)S(1)}, u32[]{:S(2)}, u32[]{:S(2)}) collective-permute-start(f32[16,128]{1,0:T(8,128)S(1)} %add.16), channel_id=1, source_target_pairs={{0,16},{4,20},{8,24},{12,28},{16,0},{20,4},{24,8},{28,12},{1,17},{... | collective-permute-start | bytes 24584 | tf_op jit(solution)/shard_map/ppermute | solution.py:301
  114.6 3.7 %collective-permute-start.26 = (f32[16,128]{1,0:T(8,128)S(1)}, f32[16,128]{1,0:T(8,128)S(1)}, u32[]{:S(2)}, u32[]{:S(2)}) collective-permute-start(f32[16,128]{1,0:T(8,128)S(1)} %add.17.inner_near), channel_id=1, source_target_pairs={{0,4},{4,0},{8,12},{12,8},{16,20},{20,16},{24,28},{28,24},{1,5},{5... | collective-permute-start | bytes 24584 | tf_op jit(solution)/shard_map/ppermute | solution.py:301
  131.1 48.6 %all-to-all-start = ((f32[8,64,128]{2,1,0:T(8,128)}), f32[8,64,128]{2,1,0:T(8,128)S(1)}, u32[]{:S(2)}, u32[]{:S(2)}) async-start(f32[8,64,128]{2,1,0:T(8,128)} %bitcast.12), calls=%async_computation | async-start | bytes 524288 | tf_op jit(solution)/shard_map/all_to_all | solution.py:683
  139.4 6.7 %collective-permute-start.20 = (bf16[528,128]{1,0:T(8,128)(2,1)}, bf16[528,128]{1,0:T(8,128)(2,1)S(1)}, u32[]{:S(2)}, u32[]{:S(2)}) collective-permute-start(bf16[528,128]{1,0:T(8,128)(2,1)} %get-tuple-element.77), channel_id=1, source_target_pairs={{0,8},{4,12},{8,0},{12,4},{16,24},{20,28},{24,16},{28,20},{1,9},{5... | collective-permute-start | bytes 405512 | tf_op jit(solution)/shard_map/ppermute | solution.py:281
  139.4 12.7 %collective-permute-start.21 = (bf16[528,128]{1,0:T(8,128)(2,1)}, bf16[528,128]{1,0:T(8,128)(2,1)S(1)}, u32[]{:S(2)}, u32[]{:S(2)}) collective-permute-start(bf16[528,128]{1,0:T(8,128)(2,1)} %get-tuple-element.78), channel_id=1, source_target_pairs={{0,16},{4,20},{8,24},{12,28},{16,0},{20,4},{24,8},{28,12},{1,17},{... | collective-permute-start | bytes 405512 | tf_op jit(solution)/shard_map/ppermute | solution.py:281
  142.3 33.8 %collective-permute-start.27 = (bf16[1040,128]{1,0:T(8,128)(2,1)S(1)}, bf16[1040,128]{1,0:T(8,128)(2,1)S(1)}, u32[]{:S(2)}, u32[]{:S(2)}) collective-permute-start(bf16[1040,128]{1,0:T(8,128)(2,1)S(1)} %copy-done.34), channel_id=1, source_target_pairs={{0,8},{4,12},{8,0},{12,4},{16,24},{20,28},{24,16},{28,20},{1,9},{5... | collective-permute-start | bytes 798728 | tf_op jit(solution)/shard_map/ppermute | solution.py:281
  143.8 32.3 %collective-permute-start.28 = (bf16[1040,128]{1,0:T(8,128)(2,1)S(1)}, bf16[1040,128]{1,0:T(8,128)(2,1)S(1)}, u32[]{:S(2)}, u32[]{:S(2)}) collective-permute-start(bf16[1040,128]{1,0:T(8,128)(2,1)S(1)} %copy-done.33), channel_id=1, source_target_pairs={{0,16},{4,20},{8,24},{12,28},{16,0},{20,4},{24,8},{28,12},{1,17},{... | collective-permute-start | bytes 798728 | tf_op jit(solution)/shard_map/ppermute | solution.py:281
  144.3 31.8 %collective-permute-start.29 = (bf16[1040,128]{1,0:T(8,128)(2,1)S(1)}, bf16[1040,128]{1,0:T(8,128)(2,1)S(1)}, u32[]{:S(2)}, u32[]{:S(2)}) collective-permute-start(bf16[1040,128]{1,0:T(8,128)(2,1)S(1)} %copy-done.32), channel_id=1, source_target_pairs={{0,24},{4,28},{8,16},{12,20},{16,8},{20,12},{24,0},{28,4},{1,25},{... | collective-permute-start | bytes 798728 | tf_op jit(solution)/shard_map/ppermute | solution.py:281
  146.0 27.2 %collective-permute-start.22 = (bf16[528,128]{1,0:T(8,128)(2,1)}, bf16[528,128]{1,0:T(8,128)(2,1)S(1)}, u32[]{:S(2)}, u32[]{:S(2)}) collective-permute-start(bf16[528,128]{1,0:T(8,128)(2,1)} %get-tuple-element.79), channel_id=1, source_target_pairs={{0,24},{4,28},{8,16},{12,20},{16,8},{20,12},{24,0},{28,4},{1,25},{... | collective-permute-start | bytes 405512 | tf_op jit(solution)/shard_map/ppermute | solution.py:281
  152.1 27.5 %collective-permute-start.30 = (bf16[528,128]{1,0:T(8,128)(2,1)}, bf16[528,128]{1,0:T(8,128)(2,1)S(1)}, u32[]{:S(2)}, u32[]{:S(2)}) collective-permute-start(bf16[528,128]{1,0:T(8,128)(2,1)} %get-tuple-element.103), channel_id=1, source_target_pairs={{0,4},{4,0},{8,12},{12,8},{16,20},{20,16},{24,28},{28,24},{1,5},{5... | collective-permute-start | bytes 405512 | tf_op jit(solution)/shard_map/ppermute | solution.py:284
  (36 other events, 147.5 us)

commit v3 on v2

--- a/solution.py
+++ b/solution.py
@@ -158,6 +158,7 @@
 
 
 OCTAVES = 240.0
+KERNEL_BYTES = 12 << 20
 LANES = 128
 
 
@@ -239,15 +240,20 @@
     return jnp.sqrt(jnp.sum(matrix * matrix, axis=1, keepdims=True) + 1e-06)
 
 
-def call(kernel, shapes, *arrays, scratch=(), smem=0):
+def call(kernel, shapes, *arrays, scratch=(), smem=0, raw=False):
     specs = [pl.BlockSpec(memory_space=pltpu.SMEM)] * smem
     specs += [pl.BlockSpec(memory_space=pltpu.VMEM)] * (len(arrays) - smem)
+    if not raw:
+        arrays = list(arrays[:smem]) + [
+            pltpu.with_memory_space_constraint(array, pltpu.VMEM) for array in arrays[smem:]
+        ]
     return pl.pallas_call(
         kernel,
-        out_shape=[jax.ShapeDtypeStruct(shape, dtype) for shape, dtype in shapes],
+        out_shape=[pltpu.VMEM(shape, dtype) for shape, dtype in shapes],
         in_specs=specs,
         out_specs=[pl.BlockSpec(memory_space=pltpu.VMEM)] * len(shapes),
         scratch_shapes=list(scratch),
+        compiler_params=pltpu.CompilerParams(vmem_limit_bytes=KERNEL_BYTES),
     )(*arrays)
 
 
@@ -306,7 +312,7 @@
     spot = jnp.stack([along_z, along_y, my_head]).astype(jnp.int32)
 
     target, kv_packed = call(
-        first_kernel, [((tokens, head_size), f32), ((size_two, LANES), bf16)], keys, values, rates
+        first_kernel, [((tokens, head_size), f32), ((size_two, LANES), bf16)], keys, values, rates, raw=True
     )
     kv_sent = gather_z(kv_packed)
 
@@ -384,6 +390,7 @@
         up_fast[0],
         down_fast[0],
         smem=1,
+        raw=True,
     )
     q_sent = gather_z(q_packed)
 

time: 183 us -> 167 us (0.913)
  Pallas kernels: 53.3 us -> 23.6 us
  local copies, waits for them, and re-layouts: 7.46 us -> 20 us
  waiting for transfers between devices: 71.3 us -> 73.4 us
  other arithmetic: 2 us -> 0.08 us
    pallas_call x14, Pallas kernels: 53.3 us -> 23.6 us  [call(): pl.pallas_call(kernel, out_shape=[pltpu.VMEM(shape, dtype) for shape, dty...]
    unnamed x72 -> x68, local copies, waits for them, and re-layouts: 7.46 us -> 20 us
    ppermute x18, waiting for transfers between devices: 42.4 us -> 45.1 us  [across(): lax.ppermute(array, 'seq', [(s, s ^ 2 * step) for s in range(seq_count)])]
    ppermute x1, waiting for transfers between devices: 13.2 us -> 11 us  [body_hidden(): og_mine = lax.ppermute(out_grad, ('seq', 'head'), perm)]
  transfers between devices with their start and end apart: 32 -> 32, of which waited for: 14 -> 15; matrix products, arithmetic and copies ran while one was open for 1% -> 1% of each run, Pallas kernels for 18% -> 8%
where the time goes in v3:
time: 167 us
  waiting for transfers between devices  73.4 us (44%)
  starting transfers between devices  48.6 us (29%)
  Pallas kernels  23.6 us (14%)
  local copies, waits for them, and re-layouts  20 us (12%)
    ppermute x18, waiting for transfers between devices, across(): lax.ppermute(array, 'seq', [(s, s ^ 2 * step) for s in range(seq_count)])  45.1 us
    pallas_call x14, Pallas kernels, call(): pl.pallas_call(kernel, out_shape=[pltpu.VMEM(shape, dtype) for shape, dty...  23.6 us
    ppermute x18, starting transfers between devices, across(): lax.ppermute(array, 'seq', [(s, s ^ 2 * step) for s in range(seq_count)])  23.5 us
    unnamed x68, local copies, waits for them, and re-layouts  20 us
    ppermute x5, waiting for transfers between devices, sum_over(): other = lax.ppermute(array, 'seq', [(s, s ^ hop) for s in range(seq_count)])  14.4 us
    ppermute x1, waiting for transfers between devices, body_hidden(): og_mine = lax.ppermute(out_grad, ('seq', 'head'), perm)  11 us
    ppermute x5, starting transfers between devices, sum_over(): other = lax.ppermute(array, 'seq', [(s, s ^ hop) for s in range(seq_count)])  9.77 us
    all_to_all x1, starting transfers between devices, body_hidden(): down_all = lax.all_to_all(down_part, 'seq', 0, 0, tiled=True)  5.84 us
  transfers between devices with their start and end apart: 32, of which 15 were waited for; matrix products, arithmetic and copies ran while one was open for 1% of the time, Pallas kernels for 8%

profile of v3, /device:TPU:10, one launch (start us, length us, event | category | flops | bytes accessed | tf_op | source)
XLA Modules:
  0.0 166.5 jit_solution(6368510026919400839)
XLA Ops:
  0.6 3.6 %collective-permute-start.7 = (bf16[128,1024]{1,0:T(8,128)(2,1)}, bf16[128,1024]{1,0:T(8,128)(2,1)S(1)}, u32[]{:S(2)}, u32[]{:S(2)}) collective-permute-start(bf16[128,1024]{1,0:T(8,128)(2,1)} %param.17), channel_id=1, source_target_pairs={{0,0},{1,8},{2,16},{3,24},{4,4},{5,12},{6,20},{7,28},{8,2},{9,10},... | collective-permute-start | bytes 786440 | tf_op jit(solution)/shard_map/ppermute | solution.py:324
  11.2 11.0 %collective-permute-done.7.refs_0_ = bf16[128,1024]{1,0:T(8,128)(2,1)S(1)} collective-permute-done((bf16[128,1024]{1,0:T(8,128)(2,1)}, bf16[128,1024]{1,0:T(8,128)(2,1)S(1)}, u32[]{:S(2)}, u32[]{:S(2)}) %collective-permute-start.7) | collective-permute-done | bytes 262176 | tf_op jit(solution)/shard_map/ppermute | solution.py:324
  22.1 5.7 %collective-permute-done.1.refs_1_ = bf16[1040,128]{1,0:T(8,128)(2,1)S(1)} collective-permute-done((bf16[1040,128]{1,0:T(8,128)(2,1)}, bf16[1040,128]{1,0:T(8,128)(2,1)S(1)}, u32[]{:S(2)}, u32[]{:S(2)}) %collective-permute-start.1) | collective-permute-done | bytes 266272 | tf_op jit(solution)/shard_map/ppermute | solution.py:287
  28.5 2.8 %collective-permute-done.9.refs_2_ = bf16[128,1024]{1,0:T(8,128)(2,1)S(1)} collective-permute-done((bf16[128,1024]{1,0:T(8,128)(2,1)S(1)}, bf16[128,1024]{1,0:T(8,128)(2,1)S(1)}, u32[]{:S(2)}, u32[]{:S(2)}) %collective-permute-start.9) | collective-permute-done | bytes 262176 | tf_op jit(solution)/shard_map/ppermute | solution.py:329
  37.3 4.0 %shard_map.138 = (bf16[512,512]{1,0:T(8,128)(2,1)S(1)}, bf16[512,512]{1,0:T(8,128)(2,1)S(1)}, bf16[512,512]{1,0:T(8,128)(2,1)S(1)}, bf16[512,512]{1,0:T(8,128)(2...) custom-call(f32[384,512]{1,0:T(8,128)S(1)} %get-tuple-element.57.weight, ...), custom_call_target="tpu_custom_call" | custom-call | tf_op jit(solution)/shard_map/pallas_call | solution.py:250
  41.3 1.6 collective-permute-start.3
  42.9 2.8 %shard_map.140 = (f32[128,512]{1,0:T(8,128)S(1)}, bf16[528,128]{1,0:T(8,128)(2,1)S(1)}, bf16[528,128]{1,0:T(8,128)(2,1)S(1)}, bf16[528,128]{1,0:T(8,128)(2,1)S(1)}) custom-call(s32[3]{0:T(128)S(1)} %pad_add_fusion.spot, bf16[512,512]{1,0:T(8,128)(2,1)S(1)} %copy-done.6, bf16[512,512]{1,0:T(8,128)(2,1)S(1)} %collective-permute-done.6.other, ...), custom_call_target="tpu_custom_call" | custom-call | tf_op jit(solution)/shard_map/pallas_call | solution.py:250
  45.8 5.1 %collective-permute-start.12 = (bf16[528,128]{1,0:T(8,128)(2,1)S(1)}, bf16[528,128]{1,0:T(8,128)(2,1)S(1)}, u32[]{:S(2)}, u32[]{:S(2)}) collective-permute-start(bf16[528,128]{1,0:T(8,128)(2,1)S(1)} %get-tuple-element.67), channel_id=1, source_target_pairs={{0,16},{4,20},{8,24},{12,28},{16,0},{20,4},{24,8},{28,12},{1,17},{... | collective-permute-start | bytes 405512 | tf_op jit(solution)/shard_map/ppermute | solution.py:287
  51.3 3.8 %collective-permute-start.15 = (bf16[528,128]{1,0:T(8,128)(2,1)S(1)}, bf16[528,128]{1,0:T(8,128)(2,1)S(1)}, u32[]{:S(2)}, u32[]{:S(2)}) collective-permute-start(bf16[528,128]{1,0:T(8,128)(2,1)S(1)} %get-tuple-element.70), channel_id=1, source_target_pairs={{0,16},{4,20},{8,24},{12,28},{16,0},{20,4},{24,8},{28,12},{1,17},{... | collective-permute-start | bytes 405512 | tf_op jit(solution)/shard_map/ppermute | solution.py:287
  55.2 7.7 %collective-permute-done.12.refs_1_ = bf16[528,128]{1,0:T(8,128)(2,1)S(1)} collective-permute-done((bf16[528,128]{1,0:T(8,128)(2,1)S(1)}, bf16[528,128]{1,0:T(8,128)(2,1)S(1)}, u32[]{:S(2)}, u32[]{:S(2)}) %collective-permute-start.12) | collective-permute-done | bytes 135200 | tf_op jit(solution)/shard_map/ppermute | solution.py:287
  62.8 4.1 %collective-permute-done.13.refs_2_ = bf16[528,128]{1,0:T(8,128)(2,1)S(1)} collective-permute-done((bf16[528,128]{1,0:T(8,128)(2,1)S(1)}, bf16[528,128]{1,0:T(8,128)(2,1)S(1)}, u32[]{:S(2)}, u32[]{:S(2)}) %collective-permute-start.13) | collective-permute-done | bytes 135200 | tf_op jit(solution)/shard_map/ppermute | solution.py:287
  67.4 2.7 %collective-permute-start.14 = (bf16[528,128]{1,0:T(8,128)(2,1)S(1)}, bf16[528,128]{1,0:T(8,128)(2,1)S(1)}, u32[]{:S(2)}, u32[]{:S(2)}) collective-permute-start(bf16[528,128]{1,0:T(8,128)(2,1)S(1)} %get-tuple-element.70), channel_id=1, source_target_pairs={{0,8},{4,12},{8,0},{12,4},{16,24},{20,28},{24,16},{28,20},{1,9},{5... | collective-permute-start | bytes 405512 | tf_op jit(solution)/shard_map/ppermute | solution.py:287
  70.2 2.2 %collective-permute-start.16 = (bf16[528,128]{1,0:T(8,128)(2,1)S(1)}, bf16[528,128]{1,0:T(8,128)(2,1)S(1)}, u32[]{:S(2)}, u32[]{:S(2)}) collective-permute-start(bf16[528,128]{1,0:T(8,128)(2,1)S(1)} %collective-permute-done.15.refs_1_), channel_id=1, source_target_pairs={{0,8},{4,12},{8,0},{12,4},{16,24},{20,28},{24,16},{28,20},{1,9},{5... | collective-permute-start | bytes 405512 | tf_op jit(solution)/shard_map/ppermute | solution.py:287
  72.4 2.4 %collective-permute-done.18.refs_4_ = bf16[528,128]{1,0:T(8,128)(2,1)S(1)} collective-permute-done((bf16[528,128]{1,0:T(8,128)(2,1)S(1)}, bf16[528,128]{1,0:T(8,128)(2,1)S(1)}, u32[]{:S(2)}, u32[]{:S(2)}) %collective-permute-start.18) | collective-permute-done | bytes 135200 | tf_op jit(solution)/shard_map/ppermute | solution.py:287
  75.5 1.8 %collective-permute-start.4 = (f32[16,128]{1,0:T(8,128)S(1)}, f32[16,128]{1,0:T(8,128)S(1)}, u32[]{:S(2)}, u32[]{:S(2)}) collective-permute-start(f32[16,128]{1,0:T(8,128)S(1)} %get-tuple-element.64), channel_id=1, source_target_pairs={{0,8},{4,12},{8,0},{12,4},{16,24},{20,28},{24,16},{28,20},{1,9},{5... | collective-permute-start | bytes 24584 | tf_op jit(solution)/shard_map/ppermute | solution.py:307
  77.3 6.0 %collective-permute-done.4 = f32[16,128]{1,0:T(8,128)S(1)} collective-permute-done((f32[16,128]{1,0:T(8,128)S(1)}, f32[16,128]{1,0:T(8,128)S(1)}, u32[]{:S(2)}, u32[]{:S(2)}) %collective-permute-start.4) | collective-permute-done | bytes 8224 | tf_op jit(solution)/shard_map/ppermute | solution.py:307
  83.3 2.2 %collective-permute-start.5 = (f32[16,128]{1,0:T(8,128)S(1)}, f32[16,128]{1,0:T(8,128)S(1)}, u32[]{:S(2)}, u32[]{:S(2)}) collective-permute-start(f32[16,128]{1,0:T(8,128)S(1)} %add.15.near), channel_id=1, source_target_pairs={{0,16},{4,20},{8,24},{12,28},{16,0},{20,4},{24,8},{28,12},{1,17},{... | collective-permute-start | bytes 24584 | tf_op jit(solution)/shard_map/ppermute | solution.py:307
  85.5 2.3 %collective-permute-done.5.far = f32[16,128]{1,0:T(8,128)S(1)} collective-permute-done((f32[16,128]{1,0:T(8,128)S(1)}, f32[16,128]{1,0:T(8,128)S(1)}, u32[]{:S(2)}, u32[]{:S(2)}) %collective-permute-start.5) | collective-permute-done | bytes 8224 | tf_op jit(solution)/shard_map/ppermute | solution.py:307
  87.8 4.4 %shard_map.142 = (f32[384,512]{1,0:T(8,128)S(1)}, bf16[1584,128]{1,0:T(8,128)(2,1)S(1)}, f32[16,128]{1,0:T(8,128)S(1)}, bf16[512,256]{1,0:T(8,128)(2,1)S(1)}, bf...) custom-call(f32[384,512]{1,0:T(8,128)S(1)} %get-tuple-element.57.weight, ...), custom_call_target="tpu_custom_call" | custom-call | tf_op jit(solution)/shard_map/pallas_call | solution.py:250
  95.6 2.1 %collective-permute-start.24 = (f32[16,128]{1,0:T(8,128)S(1)}, f32[16,128]{1,0:T(8,128)S(1)}, u32[]{:S(2)}, u32[]{:S(2)}) collective-permute-start(f32[16,128]{1,0:T(8,128)S(1)} %get-tuple-element.83), channel_id=1, source_target_pairs={{0,8},{4,12},{8,0},{12,4},{16,24},{20,28},{24,16},{28,20},{1,9},{5... | collective-permute-start | bytes 24584 | tf_op jit(solution)/shard_map/ppermute | solution.py:307
  97.7 1.6 collective-permute-done.24
  99.4 2.2 %collective-permute-start.25 = (f32[16,128]{1,0:T(8,128)S(1)}, f32[16,128]{1,0:T(8,128)S(1)}, u32[]{:S(2)}, u32[]{:S(2)}) collective-permute-start(f32[16,128]{1,0:T(8,128)S(1)} %add.16), channel_id=1, source_target_pairs={{0,16},{4,20},{8,24},{12,28},{16,0},{20,4},{24,8},{28,12},{1,17},{... | collective-permute-start | bytes 24584 | tf_op jit(solution)/shard_map/ppermute | solution.py:307
  101.5 2.4 %collective-permute-done.25 = f32[16,128]{1,0:T(8,128)S(1)} collective-permute-done((f32[16,128]{1,0:T(8,128)S(1)}, f32[16,128]{1,0:T(8,128)S(1)}, u32[]{:S(2)}, u32[]{:S(2)}) %collective-permute-start.25) | collective-permute-done | bytes 8224 | tf_op jit(solution)/shard_map/ppermute | solution.py:307
  105.4 2.1 %collective-permute-done.26.inner_far = f32[16,128]{1,0:T(8,128)S(1)} collective-permute-done((f32[16,128]{1,0:T(8,128)S(1)}, f32[16,128]{1,0:T(8,128)S(1)}, u32[]{:S(2)}, u32[]{:S(2)}) %collective-permute-start.26) | collective-permute-done | bytes 8224 | tf_op jit(solution)/shard_map/ppermute | solution.py:307
  107.6 3.7 %shard_map.145 = (bf16[384,512]{1,0:T(8,128)(2,1)S(1)}, bf16[384,512]{1,0:T(8,128)(2,1)S(1)}, f32[384,512]{1,0:T(8,128)S(1)}, bf16[512,384]{1,0:T(8,128)(2,1)S(1...) custom-call(f32[384,512]{1,0:T(8,128)S(1)} %get-tuple-element.57.wei, ...), custom_call_target="tpu_custom_call" | custom-call | tf_op jit(solution)/shard_map/pallas_call | solution.py:250
  111.3 2.1 %shard_map.146 = (f32[128,512]{1,0:T(8,128)S(1)}, f32[128,512]{1,0:T(8,128)S(1)}, bf16[128,384]{1,0:T(8,128)(2,1)S(1)}, bf16[128,384]{1,0:T(8,128)(2,1)S(1)}, f32[512,128]{1,0:T(8,128)S(1)}) custom-call(s32[3]{0:T(128)S(1)} %pad_add_fusion.spot, f32[384,512]{1,0:T(8,128)S(1)} %get-tuple-element.57.weight, f32[512,384]{1,0:T(8,128)S(1)} %get-tuple-element.80.mids, ...), custom_call_target="tpu_custom_call" | custom-call | tf_op jit(solution)/shard_map/pallas_call | solution.py:250
  114.8 5.8 %all-to-all-start = ((f32[8,64,128]{2,1,0:T(8,128)}), f32[8,64,128]{2,1,0:T(8,128)S(1)}, u32[]{:S(2)}, u32[]{:S(2)}) async-start(f32[8,64,128]{2,1,0:T(8,128)} %bitcast.12), calls=%async_computation | async-start | bytes 524288 | tf_op jit(solution)/shard_map/all_to_all | solution.py:690
  125.2 2.9 %collective-permute-start.21 = (bf16[528,128]{1,0:T(8,128)(2,1)S(1)}, bf16[528,128]{1,0:T(8,128)(2,1)S(1)}, u32[]{:S(2)}, u32[]{:S(2)}) collective-permute-start(bf16[528,128]{1,0:T(8,128)(2,1)S(1)} %get-tuple-element.78), channel_id=1, source_target_pairs={{0,16},{4,20},{8,24},{12,28},{16,0},{20,4},{24,8},{28,12},{1,17},{... | collective-permute-start | bytes 405512 | tf_op jit(solution)/shard_map/ppermute | solution.py:287
  131.6 1.6 collective-permute-done.20.refs_0_
  134.5 1.7 %shard_map.148 = (f32[128,512]{1,0:T(8,128)S(1)}, bf16[528,128]{1,0:T(8,128)(2,1)S(1)}) custom-call(s32[3]{0:T(128)S(1)} %pad_add_fusion.spot, f32[384,512]{1,0:T(8,128)S(1)} %get-tuple-element.90.directs, bf16[128,384]{1,0:T(8,128)(2,1)S(1)} %get-tuple-element.100.kept_high, bf16[128,384]{1,0:T(8,128)(2,1)S(1)} %copy-done.22, ...), custom_call_target="tpu_custom_call" | custom-call | tf_op jit(solution)/shard_map/pallas_call | solution.py:250
  137.0 1.6 collective-permute-start.30
  138.6 21.7 %collective-permute-done.22.refs_2_ = bf16[528,128]{1,0:T(8,128)(2,1)S(1)} collective-permute-done((bf16[528,128]{1,0:T(8,128)(2,1)S(1)}, bf16[528,128]{1,0:T(8,128)(2,1)S(1)}, u32[]{:S(2)}, u32[]{:S(2)}) %collective-permute-start.22) | collective-permute-done | bytes 135200 | tf_op jit(solution)/shard_map/ppermute | solution.py:287
  (118 shorter events, 37.9 us)
Async XLA Ops:
  0.6 21.5 %collective-permute-start.7 = (bf16[128,1024]{1,0:T(8,128)(2,1)}, bf16[128,1024]{1,0:T(8,128)(2,1)S(1)}, u32[]{:S(2)}, u32[]{:S(2)}) collective-permute-start(bf16[128,1024]{1,0:T(8,128)(2,1)} %param.17), channel_id=1, source_target_pairs={{0,0},{1,8},{2,16},{3,24},{4,4},{5,12},{6,20},{7,28},{8,2},{9,10},... | collective-permute-start | bytes 786440 | tf_op jit(solution)/shard_map/ppermute | solution.py:324
  8.6 19.3 %collective-permute-start.1 = (bf16[1040,128]{1,0:T(8,128)(2,1)}, bf16[1040,128]{1,0:T(8,128)(2,1)S(1)}, u32[]{:S(2)}, u32[]{:S(2)}) collective-permute-start(bf16[1040,128]{1,0:T(8,128)(2,1)} %get-tuple-element.60), channel_id=1, source_target_pairs={{0,16},{4,20},{8,24},{12,28},{16,0},{20,4},{24,8},{28,12},{1,17},{... | collective-permute-start | bytes 798728 | tf_op jit(solution)/shard_map/ppermute | solution.py:287
  9.7 33.2 %collective-permute-start.6 = (bf16[512,512]{1,0:T(8,128)(2,1)}, bf16[512,512]{1,0:T(8,128)(2,1)S(1)}, u32[]{:S(2)}, u32[]{:S(2)}) collective-permute-start(bf16[512,512]{1,0:T(8,128)(2,1)} %mine.1), channel_id=1, source_target_pairs={{0,4},{4,0},{8,12},{12,8},{16,20},{20,16},{24,28},{28,24},{1,5},{5... | collective-permute-start | bytes 1572872 | tf_op jit(solution)/shard_map/ppermute | solution.py:290
  22.1 9.2 %collective-permute-start.9 = (bf16[128,1024]{1,0:T(8,128)(2,1)S(1)}, bf16[128,1024]{1,0:T(8,128)(2,1)S(1)}, u32[]{:S(2)}, u32[]{:S(2)}) collective-permute-start(bf16[128,1024]{1,0:T(8,128)(2,1)S(1)} %collective-permute-done.7.refs_0_), channel_id=1, source_target_pairs={{0,2},{1,3},{2,0},{3,1},{4,6},{5,7},{6,4},{7,5},{8,10},{9,11},{10,... | collective-permute-start | bytes 786440 | tf_op jit(solution)/shard_map/ppermute | solution.py:329
  22.1 14.0 %collective-permute-start = (bf16[1040,128]{1,0:T(8,128)(2,1)}, bf16[1040,128]{1,0:T(8,128)(2,1)S(1)}, u32[]{:S(2)}, u32[]{:S(2)}) collective-permute-start(bf16[1040,128]{1,0:T(8,128)(2,1)} %get-tuple-element.60), channel_id=1, source_target_pairs={{0,8},{4,12},{8,0},{12,4},{16,24},{20,28},{24,16},{28,20},{1,9},{5... | collective-permute-start | bytes 798728 | tf_op jit(solution)/shard_map/ppermute | solution.py:287
  27.9 9.4 %collective-permute-start.2 = (bf16[1040,128]{1,0:T(8,128)(2,1)S(1)}, bf16[1040,128]{1,0:T(8,128)(2,1)S(1)}, u32[]{:S(2)}, u32[]{:S(2)}) collective-permute-start(bf16[1040,128]{1,0:T(8,128)(2,1)S(1)} %collective-permute-done.1.refs_1_), channel_id=1, source_target_pairs={{0,8},{4,12},{8,0},{12,4},{16,24},{20,28},{24,16},{28,20},{1,9},{5... | collective-permute-start | bytes 798728 | tf_op jit(solution)/shard_map/ppermute | solution.py:287
  27.9 15.0 %collective-permute-start.8 = (bf16[128,1024]{1,0:T(8,128)(2,1)S(1)}, bf16[128,1024]{1,0:T(8,128)(2,1)S(1)}, u32[]{:S(2)}, u32[]{:S(2)}) collective-permute-start(bf16[128,1024]{1,0:T(8,128)(2,1)S(1)} %collective-permute-done.7.refs_0_), channel_id=1, source_target_pairs={{0,1},{1,0},{2,3},{3,2},{4,5},{5,4},{6,7},{7,6},{8,9},{9,8},{10,11... | collective-permute-start | bytes 786440 | tf_op jit(solution)/shard_map/ppermute | solution.py:329
  31.3 11.6 %collective-permute-start.10 = (bf16[128,1024]{1,0:T(8,128)(2,1)S(1)}, bf16[128,1024]{1,0:T(8,128)(2,1)}, u32[]{:S(2)}, u32[]{:S(2)}) collective-permute-start(bf16[128,1024]{1,0:T(8,128)(2,1)S(1)} %collective-permute-done.9.refs_2_), channel_id=1, source_target_pairs={{0,1},{1,0},{2,3},{3,2},{4,5},{5,4},{6,7},{7,6},{8,9},{9,8},{10,11... | collective-permute-start | bytes 786440 | tf_op jit(solution)/shard_map/ppermute | solution.py:329
  41.3 33.7 %collective-permute-start.3 = (bf16[1584,128]{1,0:T(8,128)(2,1)S(1)}, bf16[1584,128]{1,0:T(8,128)(2,1)S(1)}, u32[]{:S(2)}, u32[]{:S(2)}) collective-permute-start(bf16[1584,128]{1,0:T(8,128)(2,1)S(1)} %get-tuple-element.62), channel_id=1, source_target_pairs={{0,4},{4,0},{8,12},{12,8},{16,20},{20,16},{24,28},{28,24},{1,5},{5... | collective-permute-start | bytes 1216520 | tf_op jit(solution)/shard_map/ppermute | solution.py:290
  45.7 9.5 %collective-permute-start.11 = (bf16[528,128]{1,0:T(8,128)(2,1)S(1)}, bf16[528,128]{1,0:T(8,128)(2,1)S(1)}, u32[]{:S(2)}, u32[]{:S(2)}) collective-permute-start(bf16[528,128]{1,0:T(8,128)(2,1)S(1)} %get-tuple-element.66), channel_id=1, source_target_pairs={{0,8},{4,12},{8,0},{12,4},{16,24},{20,28},{24,16},{28,20},{1,9},{5... | collective-permute-start | bytes 405512 | tf_op jit(solution)/shard_map/ppermute | solution.py:287
  45.8 17.0 %collective-permute-start.12 = (bf16[528,128]{1,0:T(8,128)(2,1)S(1)}, bf16[528,128]{1,0:T(8,128)(2,1)S(1)}, u32[]{:S(2)}, u32[]{:S(2)}) collective-permute-start(bf16[528,128]{1,0:T(8,128)(2,1)S(1)} %get-tuple-element.67), channel_id=1, source_target_pairs={{0,16},{4,20},{8,24},{12,28},{16,0},{20,4},{24,8},{28,12},{1,17},{... | collective-permute-start | bytes 405512 | tf_op jit(solution)/shard_map/ppermute | solution.py:287
  50.8 16.1 %collective-permute-start.13 = (bf16[528,128]{1,0:T(8,128)(2,1)S(1)}, bf16[528,128]{1,0:T(8,128)(2,1)S(1)}, u32[]{:S(2)}, u32[]{:S(2)}) collective-permute-start(bf16[528,128]{1,0:T(8,128)(2,1)S(1)} %get-tuple-element.68), channel_id=1, source_target_pairs={{0,24},{4,28},{8,16},{12,20},{16,8},{20,12},{24,0},{28,4},{1,25},{... | collective-permute-start | bytes 405512 | tf_op jit(solution)/shard_map/ppermute | solution.py:287
  51.3 18.9 %collective-permute-start.15 = (bf16[528,128]{1,0:T(8,128)(2,1)S(1)}, bf16[528,128]{1,0:T(8,128)(2,1)S(1)}, u32[]{:S(2)}, u32[]{:S(2)}) collective-permute-start(bf16[528,128]{1,0:T(8,128)(2,1)S(1)} %get-tuple-element.70), channel_id=1, source_target_pairs={{0,16},{4,20},{8,24},{12,28},{16,0},{20,4},{24,8},{28,12},{1,17},{... | collective-permute-start | bytes 405512 | tf_op jit(solution)/shard_map/ppermute | solution.py:287
  67.4 7.4 %collective-permute-start.18 = (bf16[528,128]{1,0:T(8,128)(2,1)S(1)}, bf16[528,128]{1,0:T(8,128)(2,1)S(1)}, u32[]{:S(2)}, u32[]{:S(2)}) collective-permute-start(bf16[528,128]{1,0:T(8,128)(2,1)S(1)} %get-tuple-element.71), channel_id=1, source_target_pairs={{0,16},{4,20},{8,24},{12,28},{16,0},{20,4},{24,8},{28,12},{1,17},{... | collective-permute-start | bytes 405512 | tf_op jit(solution)/shard_map/ppermute | solution.py:287
  67.4 18.1 %collective-permute-start.14 = (bf16[528,128]{1,0:T(8,128)(2,1)S(1)}, bf16[528,128]{1,0:T(8,128)(2,1)S(1)}, u32[]{:S(2)}, u32[]{:S(2)}) collective-permute-start(bf16[528,128]{1,0:T(8,128)(2,1)S(1)} %get-tuple-element.70), channel_id=1, source_target_pairs={{0,8},{4,12},{8,0},{12,4},{16,24},{20,28},{24,16},{28,20},{1,9},{5... | collective-permute-start | bytes 405512 | tf_op jit(solution)/shard_map/ppermute | solution.py:287
  70.2 15.3 %collective-permute-start.16 = (bf16[528,128]{1,0:T(8,128)(2,1)S(1)}, bf16[528,128]{1,0:T(8,128)(2,1)S(1)}, u32[]{:S(2)}, u32[]{:S(2)}) collective-permute-start(bf16[528,128]{1,0:T(8,128)(2,1)S(1)} %collective-permute-done.15.refs_1_), channel_id=1, source_target_pairs={{0,8},{4,12},{8,0},{12,4},{16,24},{20,28},{24,16},{28,20},{1,9},{5... | collective-permute-start | bytes 405512 | tf_op jit(solution)/shard_map/ppermute | solution.py:287
  72.3 15.5 %collective-permute-start.17 = (bf16[528,128]{1,0:T(8,128)(2,1)S(1)}, bf16[528,128]{1,0:T(8,128)(2,1)S(1)}, u32[]{:S(2)}, u32[]{:S(2)}) collective-permute-start(bf16[528,128]{1,0:T(8,128)(2,1)S(1)} %get-tuple-element.71), channel_id=1, source_target_pairs={{0,8},{4,12},{8,0},{12,4},{16,24},{20,28},{24,16},{28,20},{1,9},{5... | collective-permute-start | bytes 405512 | tf_op jit(solution)/shard_map/ppermute | solution.py:287
  74.8 13.0 %collective-permute-start.19 = (bf16[528,128]{1,0:T(8,128)(2,1)S(1)}, bf16[528,128]{1,0:T(8,128)(2,1)S(1)}, u32[]{:S(2)}, u32[]{:S(2)}) collective-permute-start(bf16[528,128]{1,0:T(8,128)(2,1)S(1)} %collective-permute-done.18.refs_4_), channel_id=1, source_target_pairs={{0,8},{4,12},{8,0},{12,4},{16,24},{20,28},{24,16},{28,20},{1,9},{5... | collective-permute-start | bytes 405512 | tf_op jit(solution)/shard_map/ppermute | solution.py:287
  75.5 7.7 %collective-permute-start.4 = (f32[16,128]{1,0:T(8,128)S(1)}, f32[16,128]{1,0:T(8,128)S(1)}, u32[]{:S(2)}, u32[]{:S(2)}) collective-permute-start(f32[16,128]{1,0:T(8,128)S(1)} %get-tuple-element.64), channel_id=1, source_target_pairs={{0,8},{4,12},{8,0},{12,4},{16,24},{20,28},{24,16},{28,20},{1,9},{5... | collective-permute-start | bytes 24584 | tf_op jit(solution)/shard_map/ppermute | solution.py:307
  83.3 4.5 %collective-permute-start.5 = (f32[16,128]{1,0:T(8,128)S(1)}, f32[16,128]{1,0:T(8,128)S(1)}, u32[]{:S(2)}, u32[]{:S(2)}) collective-permute-start(f32[16,128]{1,0:T(8,128)S(1)} %add.15.near), channel_id=1, source_target_pairs={{0,16},{4,20},{8,24},{12,28},{16,0},{20,4},{24,8},{28,12},{1,17},{... | collective-permute-start | bytes 24584 | tf_op jit(solution)/shard_map/ppermute | solution.py:307
  95.1 12.5 %collective-permute-start.23 = (bf16[1584,128]{1,0:T(8,128)(2,1)S(1)}, bf16[1584,128]{1,0:T(8,128)(2,1)S(1)}, u32[]{:S(2)}, u32[]{:S(2)}) collective-permute-start(bf16[1584,128]{1,0:T(8,128)(2,1)S(1)} %get-tuple-element.82), channel_id=1, source_target_pairs={{0,4},{4,0},{8,12},{12,8},{16,20},{20,16},{24,28},{28,24},{1,5},{5... | collective-permute-start | bytes 1216520 | tf_op jit(solution)/shard_map/ppermute | solution.py:290
  95.6 3.7 %collective-permute-start.24 = (f32[16,128]{1,0:T(8,128)S(1)}, f32[16,128]{1,0:T(8,128)S(1)}, u32[]{:S(2)}, u32[]{:S(2)}) collective-permute-start(f32[16,128]{1,0:T(8,128)S(1)} %get-tuple-element.83), channel_id=1, source_target_pairs={{0,8},{4,12},{8,0},{12,4},{16,24},{20,28},{24,16},{28,20},{1,9},{5... | collective-permute-start | bytes 24584 | tf_op jit(solution)/shard_map/ppermute | solution.py:307
  99.4 4.5 %collective-permute-start.25 = (f32[16,128]{1,0:T(8,128)S(1)}, f32[16,128]{1,0:T(8,128)S(1)}, u32[]{:S(2)}, u32[]{:S(2)}) collective-permute-start(f32[16,128]{1,0:T(8,128)S(1)} %add.16), channel_id=1, source_target_pairs={{0,16},{4,20},{8,24},{12,28},{16,0},{20,4},{24,8},{28,12},{1,17},{... | collective-permute-start | bytes 24584 | tf_op jit(solution)/shard_map/ppermute | solution.py:307
  103.9 3.7 %collective-permute-start.26 = (f32[16,128]{1,0:T(8,128)S(1)}, f32[16,128]{1,0:T(8,128)S(1)}, u32[]{:S(2)}, u32[]{:S(2)}) collective-permute-start(f32[16,128]{1,0:T(8,128)S(1)} %add.17.inner_near), channel_id=1, source_target_pairs={{0,4},{4,0},{8,12},{12,8},{16,20},{20,16},{24,28},{28,24},{1,5},{5... | collective-permute-start | bytes 24584 | tf_op jit(solution)/shard_map/ppermute | solution.py:307
  114.8 49.3 %all-to-all-start = ((f32[8,64,128]{2,1,0:T(8,128)}), f32[8,64,128]{2,1,0:T(8,128)S(1)}, u32[]{:S(2)}, u32[]{:S(2)}) async-start(f32[8,64,128]{2,1,0:T(8,128)} %bitcast.12), calls=%async_computation | async-start | bytes 524288 | tf_op jit(solution)/shard_map/all_to_all | solution.py:690
  125.2 8.0 %collective-permute-start.20 = (bf16[528,128]{1,0:T(8,128)(2,1)S(1)}, bf16[528,128]{1,0:T(8,128)(2,1)S(1)}, u32[]{:S(2)}, u32[]{:S(2)}) collective-permute-start(bf16[528,128]{1,0:T(8,128)(2,1)S(1)} %get-tuple-element.77), channel_id=1, source_target_pairs={{0,8},{4,12},{8,0},{12,4},{16,24},{20,28},{24,16},{28,20},{1,9},{5... | collective-permute-start | bytes 405512 | tf_op jit(solution)/shard_map/ppermute | solution.py:287
  125.2 11.8 %collective-permute-start.21 = (bf16[528,128]{1,0:T(8,128)(2,1)S(1)}, bf16[528,128]{1,0:T(8,128)(2,1)S(1)}, u32[]{:S(2)}, u32[]{:S(2)}) collective-permute-start(bf16[528,128]{1,0:T(8,128)(2,1)S(1)} %get-tuple-element.78), channel_id=1, source_target_pairs={{0,16},{4,20},{8,24},{12,28},{16,0},{20,4},{24,8},{28,12},{1,17},{... | collective-permute-start | bytes 405512 | tf_op jit(solution)/shard_map/ppermute | solution.py:287
  128.2 33.2 %collective-permute-start.27 = (bf16[1040,128]{1,0:T(8,128)(2,1)S(1)}, bf16[1040,128]{1,0:T(8,128)(2,1)S(1)}, u32[]{:S(2)}, u32[]{:S(2)}) collective-permute-start(bf16[1040,128]{1,0:T(8,128)(2,1)S(1)} %copy-done.30), channel_id=1, source_target_pairs={{0,8},{4,12},{8,0},{12,4},{16,24},{20,28},{24,16},{28,20},{1,9},{5... | collective-permute-start | bytes 798728 | tf_op jit(solution)/shard_map/ppermute | solution.py:287
  129.6 31.7 %collective-permute-start.28 = (bf16[1040,128]{1,0:T(8,128)(2,1)S(1)}, bf16[1040,128]{1,0:T(8,128)(2,1)S(1)}, u32[]{:S(2)}, u32[]{:S(2)}) collective-permute-start(bf16[1040,128]{1,0:T(8,128)(2,1)S(1)} %copy-done.28), channel_id=1, source_target_pairs={{0,16},{4,20},{8,24},{12,28},{16,0},{20,4},{24,8},{28,12},{1,17},{... | collective-permute-start | bytes 798728 | tf_op jit(solution)/shard_map/ppermute | solution.py:287
  130.2 31.1 %collective-permute-start.29 = (bf16[1040,128]{1,0:T(8,128)(2,1)S(1)}, bf16[1040,128]{1,0:T(8,128)(2,1)S(1)}, u32[]{:S(2)}, u32[]{:S(2)}) collective-permute-start(bf16[1040,128]{1,0:T(8,128)(2,1)S(1)} %copy-done.26), channel_id=1, source_target_pairs={{0,24},{4,28},{8,16},{12,20},{16,8},{20,12},{24,0},{28,4},{1,25},{... | collective-permute-start | bytes 798728 | tf_op jit(solution)/shard_map/ppermute | solution.py:287
  133.2 27.1 %collective-permute-start.22 = (bf16[528,128]{1,0:T(8,128)(2,1)S(1)}, bf16[528,128]{1,0:T(8,128)(2,1)S(1)}, u32[]{:S(2)}, u32[]{:S(2)}) collective-permute-start(bf16[528,128]{1,0:T(8,128)(2,1)S(1)} %get-tuple-element.79), channel_id=1, source_target_pairs={{0,24},{4,28},{8,16},{12,20},{16,8},{20,12},{24,0},{28,4},{1,25},{... | collective-permute-start | bytes 405512 | tf_op jit(solution)/shard_map/ppermute | solution.py:287
  137.0 27.1 %collective-permute-start.30 = (bf16[528,128]{1,0:T(8,128)(2,1)S(1)}, bf16[528,128]{1,0:T(8,128)(2,1)S(1)}, u32[]{:S(2)}, u32[]{:S(2)}) collective-permute-start(bf16[528,128]{1,0:T(8,128)(2,1)S(1)} %get-tuple-element.103), channel_id=1, source_target_pairs={{0,4},{4,0},{8,12},{12,8},{16,20},{20,16},{24,28},{28,24},{1,5},{5... | collective-permute-start | bytes 405512 | tf_op jit(solution)/shard_map/ppermute | solution.py:290
  (31 other events, 112.8 us)
